TPU v7x, 32 devices: a whole 2x2x4 slice. The times are simulated.
32 devices in a mesh: ctx: 8 (over z, x), ch: 4 (over y, core).
Axes of the slice: x: 2, y: 2, z: 4, core: 2. Of those that a mesh axis runs over, the one named last changes fastest.
Arguments:
- short_conv_input: bfloat16 [1024, 1024], P('ctx', 'ch'), may hold values from -6 to 6
- out_gate: bfloat16 [1024, 1024], P('ctx', 'ch'), may hold values from -6 to 6
- in_gate: bfloat16 [1024, 1024], P('ctx', 'ch'), may hold values from -6 to 6
- out_cotangent: bfloat16 [1024, 1024], P('ctx', 'ch'), may hold values from -6 to 6
- mr_filter: bfloat16 [128, 64], P(None, 'ch'), may hold values from -0.5 to 0.5
- residues: float32 [16, 1024], P(None, ('ch', 'ctx')), may hold values from -5 to 5
- rates: float32 [16, 1024], P(None, ('ch', 'ctx')), may hold values from 0.0009765625 to 0.03
Outputs:
- input_grad: bfloat16 [1024, 1024], P('ctx', 'ch')
- out_gate_grad: bfloat16 [1024, 1024], P('ctx', 'ch')
- in_gate_grad: bfloat16 [1024, 1024], P('ctx', 'ch')
- filter_grad: float32 [128, 64], P(None, 'ch')
- residue_grad: float32 [16, 1024], P(None, ('ch', 'ctx'))
- rate_grad: float32 [16, 1024], P(None, ('ch', 'ctx'))
All inputs are finite; a program needn't handle non-finite values.
Results may differ from a plain program's by a relative error of at most 0.013.
Values may be sent and summed in bfloat16 or wider, within the bound.
A program may use at most 64 MiB of HBM per device.

v0:
```python
import functools
import math

import jax
import jax.numpy as jnp
import numpy as np
from jax import lax
from jax.experimental import pallas as pl
from jax.experimental.pallas import tpu as pltpu
from jax.sharding import PartitionSpec as P

MESH = pl.DeviceIdType.MESH
F32, BF16 = jnp.float32, jnp.bfloat16
AXIS = "ctx"
GRANT = 60 * 1024 * 1024


def dft_tables(half):
    size = 2 * half
    k = np.arange(half)[:, None]
    t = np.arange(half)[None, :]
    angle = 2.0 * np.pi * (k * t % size) / size
    real, imag = np.cos(angle), -np.sin(angle)
    imag[0] = np.cos(np.pi * np.arange(half))
    forward = np.concatenate([real, imag], axis=0)
    gain = np.full((size, 1), 2.0 / size)
    gain[0] = gain[half] = 1.0 / size
    inverse = (forward * gain).T

    def split(table):
        table = table.astype(np.float32)
        high = table.astype(BF16)
        return high, (table - high.astype(np.float32)).astype(BF16)

    return np.concatenate(split(forward), axis=1), np.concatenate(split(inverse), axis=0)


def dot(left, right):
    return jnp.dot(left, right, preferred_element_type=F32)


def split(value):
    high = value.astype(BF16)
    return high, (value - high.astype(F32)).astype(BF16)


def product(left, right):
    return (left.astype(F32) * right.astype(F32)).astype(BF16)


def kernel(
    n, x_hbm, og_hbm, ig_hbm, oc_hbm, filt_hbm, res_hbm, rate_hbm, fwd_hbm, inv_hbm,
    xg_ref, ogg_ref, igg_ref, fg_ref, rg_ref, tg_ref, rim, rr_all, d_all, u_all, dv, dv_rim, mp_send, mp_all, fg_all,
    rates, resid, decay, decay_rev, coef, h_ref, d_sum, u_sum, m_sum, dz_ref, u_ref, g_ref,
    back_ref, conv_ref, xs_ref, fs_ref, mr_ref,
    x_ref, og_ref, ig_ref, oc_ref, filt_ref, res_ref, rate_ref, fwd_ref, inv_ref, in_sem,
    rim_sem, rr_send, rr_recv, d_send, d_recv, u_send, u_recv, dv_sem, mp_ssem, mp_rsem, fg_send, fg_recv,
):
    order = (
        (rate_hbm, rate_ref), (res_hbm, res_ref), (x_hbm, x_ref), (filt_hbm, filt_ref), (fwd_hbm, fwd_ref),
        (og_hbm, og_ref), (oc_hbm, oc_ref), (ig_hbm, ig_ref), (inv_hbm, inv_ref),
    )
    loads = [pltpu.make_async_copy(src, dst, in_sem.at[i]) for i, (src, dst) in enumerate(order)]
    for load in loads:
        load.start()
    me = lax.axis_index(AXIS)
    rows, chans = x_ref.shape
    modes, own = rate_ref.shape
    groups = filt_ref.shape[0]
    parts = modes // 8

    barrier = pltpu.get_barrier_semaphore()

    def greet(k, carry):
        pl.semaphore_signal(barrier, inc=1, device_id={AXIS: lax.rem(me + k, n)}, device_id_type=MESH)
        return carry

    lax.fori_loop(1, n, greet, 0)
    loads[0].wait()
    loads[1].wait()
    for g in range(parts):
        rr_all[me, :, g * own : (g + 1) * own] = rate_ref[8 * g : 8 * g + 8, :]
        rr_all[me, :, (parts + g) * own : (parts + g + 1) * own] = res_ref[8 * g : 8 * g + 8, :]
    pl.semaphore_wait(barrier, n - 1)

    def remote(src, dst, ssem, rsem, to):
        return pltpu.make_async_remote_copy(
            src_ref=src, dst_ref=dst, send_sem=ssem, recv_sem=rsem, device_id={AXIS: to}, device_id_type=MESH
        )

    def rr_copy(slot, to):
        return remote(rr_all.at[slot], rr_all.at[slot], rr_send.at[to], rr_recv.at[slot], to)

    def fg_copy(slot, to):
        return remote(fg_all.at[slot], fg_all.at[slot], fg_send.at[to], fg_recv.at[slot], to)

    def mp_copy(slot, to):
        return remote(mp_send.at[to], mp_all.at[slot], mp_ssem.at[to], mp_rsem.at[slot], to)

    def d_copy(slot, to):
        return remote(d_all.at[slot], d_all.at[slot], d_send.at[to], d_recv.at[slot], to)

    def u_copy(slot, to):
        return remote(u_all.at[slot], u_all.at[slot], u_send.at[to], u_recv.at[slot], to)

    def rim_copy(to):
        return remote(x_ref, rim, rim_sem.at[0], rim_sem.at[1], to)

    def dv_copy(to):
        return remote(dv, dv_rim, dv_sem.at[0], dv_sem.at[1], to)

    def others(act):
        def step(k, carry):
            act(lax.rem(me + k, n))
            return carry

        lax.fori_loop(1, n, step, 0)

    def span(lo, hi, act):
        def step(j, carry):
            act(j)
            return carry

        lax.fori_loop(lo, hi, step, 0)

    others(lambda j: rr_copy(me, j).start())
    loads[2].wait()

    @pl.when(me < n - 1)
    def _():
        rim_copy(me + 1).start()

    for load in loads[3:]:
        load.wait()
    fwd = fwd_ref[...]
    fwd_hi = fwd[:, :rows]
    inv_hi = inv_ref[:rows, :]
    inv_lo = inv_ref[rows:, :]
    tau = lax.broadcasted_iota(jnp.int32, (rows, chans), 0)
    first_row = tau == 0
    sign = (1 - 2 * lax.rem(lax.broadcasted_iota(jnp.int32, (2 * rows, chans), 0), 2)).astype(F32)

    def spectrum(value):
        return dot(fwd, jnp.concatenate([value, value], axis=0))

    def signal(spec):
        high, low = split(spec)
        return dot(inv_hi, high) + dot(inv_hi, low) + dot(inv_lo, high)

    def times(a, b, conj):
        ar, ai, br, bi = a[:rows], a[rows:], b[:rows], b[rows:]
        pure = ai * bi
        cross = jnp.where(first_row, 0.0, pure)
        if conj:
            return jnp.concatenate([ar * br + cross, jnp.where(first_row, pure, ar * bi - ai * br)], axis=0)
        return jnp.concatenate([ar * br - cross, jnp.where(first_row, pure, ar * bi + ai * br)], axis=0)

    member = (
        lax.broadcasted_iota(jnp.int32, (groups, chans), 1) // (chans // groups)
        == lax.broadcasted_iota(jnp.int32, (groups, chans), 0)
    ).astype(BF16)
    taps = lax.dot_general(
        filt_ref[...], member, (((0,), (0,)), ((), ())), preferred_element_type=F32
    ).astype(BF16)
    fs_ref[...] = spectrum(taps)
    dz = product(og_ref[...], oc_ref[...])
    dz_ref[...] = dz.astype(F32)
    xs_ref[...] = spectrum(x_ref[...])

    others(lambda j: rr_copy(j, j).wait_recv())
    for j in range(n):
        piece = rr_all[j]
        for g in range(parts):
            rates[8 * g : 8 * g + 8, j * own : (j + 1) * own] = piece[:, g * own : (g + 1) * own]
            resid[8 * g : 8 * g + 8, j * own : (j + 1) * own] = piece[:, (parts + g) * own : (parts + g + 1) * own]

    norm = jnp.sqrt(2.0 * rates[...] / modes)
    resid[...] = resid[...] * norm
    tiles = rows // 8
    low = lax.broadcasted_iota(jnp.int32, (8, chans), 0).astype(F32)
    high = 7.0 - low
    batch = 4

    def put_moments(sums, m, first, second):
        sums[pl.ds(m, 1), :] = jnp.sum(first, axis=0, keepdims=True)
        sums[pl.ds(modes + m, 1), :] = jnp.sum(second, axis=0, keepdims=True)

    def build(group, carry):
        for i in range(batch):
            m = group * batch + i
            rate = jnp.broadcast_to(rates[pl.ds(m, 1), :], (8, chans))
            hop = jnp.exp(-8.0 * rate)
            e = jnp.exp(-rate * low)
            e_rev = jnp.exp(-rate * high)
            first = run = jnp.zeros((8, chans), F32)
            for t in range(tiles):
                decay[m, 8 * t : 8 * t + 8, :] = e
                decay_rev[m, rows - 8 * t - 8 : rows - 8 * t, :] = e_rev
                first += e * dz_ref[8 * t : 8 * t + 8, :]
                if t < tiles - 1:
                    run += first
                    e, e_rev = e * hop, e_rev * hop
            put_moments(d_sum, m, first, 8.0 * ((tiles - 1) * first - run) + low * first)
        return carry

    lax.fori_loop(0, modes // batch, build, 0)

    def moments(sums, table, value, back):
        def step(group, carry):
            first = [jnp.zeros((8, chans), F32)] * batch
            run = list(first)
            for t in range(tiles):
                part = value[8 * t : 8 * t + 8, :]
                for i in range(batch):
                    first[i] += table[group * batch + i, 8 * t : 8 * t + 8, :] * part
                    if t < tiles - 1:
                        run[i] += first[i]
            for i in range(batch):
                if back:
                    second = 8.0 * run[i] + high * first[i]
                else:
                    second = 8.0 * ((tiles - 1) * first[i] - run[i]) + low * first[i]
                put_moments(sums, group * batch + i, first[i], second)
            return carry

        lax.fori_loop(0, modes // batch, step, 0)

    def blend(weight, table, at):
        parts = [weight[m : m + 1, :] * table[m, at, :] for m in range(modes)]
        while len(parts) > 1:
            parts = [left + right for left, right in zip(parts[::2], parts[1::2])]
        return parts[0]

    def blocks(act):
        def step(i, carry):
            act(pl.ds(pl.multiple_of(16 * i, 16), 16))
            return carry

        lax.fori_loop(0, rows // 16, step, 0)

    d_all[me] = d_sum[:modes, :].astype(BF16)
    span(0, me, lambda j: d_copy(me, j).start())

    @pl.when(me == 0)
    def _():
        rim[...] = jnp.zeros_like(rim)

    @pl.when(me > 0)
    def _():
        rim_copy(me).wait_recv()

    xs = xs_ref[...] + sign * spectrum(rim[...])
    xs_ref[...] = xs
    mr = signal(times(fs_ref[...], xs, False)).astype(BF16)
    mr_ref[...] = mr
    u = product(ig_ref[...], mr)
    u_ref[...] = u.astype(F32)

    moments(u_sum, decay_rev, u_ref, True)
    u_all[me] = u_sum[:modes, :].astype(BF16)
    span(me + 1, n, lambda j: u_copy(me, j).start())

    def fill(at):
        h_ref[at, :] = blend(resid, decay, at)

    blocks(fill)
    h_hi, h_lo = split(h_ref[...])
    hs = spectrum(h_hi) + dot(fwd_hi, h_lo)
    us = spectrum(u)
    ds = spectrum(dz)
    back_ref[...] = signal(times(hs, ds, True))
    g_ref[...] = signal(times(us, ds, True))
    moments(m_sum, decay, g_ref, False)

    step_decay = jnp.exp(-rates[...])
    jump = jnp.exp(-rates[...] * rows)

    span(me + 1, n, lambda j: d_copy(j, j).wait_recv())
    later = lax.fori_loop(
        0, n - 1 - me, lambda i, b: b * jump + d_all[n - 1 - i].astype(F32), jnp.zeros((modes, chans), F32)
    )
    coef[...] = resid[...] * step_decay * later

    def gates(at):
        back = (back_ref[at, :] + blend(coef, decay_rev, at)).astype(BF16)
        dv[at, :] = product(back, ig_ref[at, :])
        igg_ref[at, :] = product(back, mr_ref[at, :])

    blocks(gates)

    @pl.when(me > 0)
    def _():
        dv_copy(me - 1).start()

    dvs = spectrum(dv[...])
    c_hi, c_lo = split(signal(times(xs_ref[...], dvs, True)))
    nt = (((1,), (1,)), ((), ()))
    fg_all[me] = (
        lax.dot_general(member, c_hi, nt, preferred_element_type=F32)
        + lax.dot_general(member, c_lo, nt, preferred_element_type=F32)
    ).astype(BF16)
    others(lambda j: fg_copy(me, j).start())

    conv_ref[...] = signal(times(hs, us, False))
    span(0, me, lambda j: u_copy(j, j).wait_recv())

    def prior(j, carry):
        s, far = carry
        return s * jump + u_all[j].astype(F32), (far + s) * jump

    zero = jnp.zeros((modes, chans), F32)
    s, far = lax.fori_loop(0, me, prior, (zero, zero))
    s = s * step_decay
    d0, d1 = d_sum[:modes, :], d_sum[modes:, :]
    m_sum[:modes, :] += s * d0
    m_sum[modes:, :] += s * (d0 + d1) + step_decay * (rows * far * d0 + u_sum[modes:, :] * later)
    for j in range(n):
        for g in range(2 * parts):
            mp_send[j, :, g * own : (g + 1) * own] = m_sum[8 * g : 8 * g + 8, j * own : (j + 1) * own]
    mp_all[me] = mp_send[me]
    others(lambda j: mp_copy(me, j).start())

    coef[...] = resid[...] * s

    def emit(at):
        conv = (conv_ref[at, :] + blend(coef, decay, at)).astype(BF16)
        ogg_ref[at, :] = product(oc_ref[at, :], conv)

    blocks(emit)

    @pl.when(me == n - 1)
    def _():
        dv_rim[...] = jnp.zeros_like(dv_rim)

    @pl.when(me < n - 1)
    def _():
        dv_copy(me).wait_recv()

    ws = dvs + sign * spectrum(dv_rim[...])
    xg_ref[...] = signal(times(fs_ref[...], ws, True)).astype(BF16)

    scale = 1.0 / math.sqrt(rows * n)
    others(lambda j: fg_copy(j, j).wait_recv())
    fg_ref[...] = jnp.sum(fg_all[...].astype(F32), axis=0) * scale
    others(lambda j: mp_copy(j, j).wait_recv())
    total = jnp.sum(mp_all[...], axis=0)
    for g in range(parts):
        rate = rate_ref[8 * g : 8 * g + 8, :]
        gain = jnp.sqrt(2.0 * rate / modes)
        first = total[:, g * own : (g + 1) * own]
        second = total[:, (parts + g) * own : (parts + g + 1) * own]
        rg_ref[8 * g : 8 * g + 8, :] = gain * first * scale
        tg_ref[8 * g : 8 * g + 8, :] = res_ref[8 * g : 8 * g + 8, :] * gain * (0.5 * first - rate * second) * scale

    others(lambda j: rr_copy(me, j).wait_send())
    others(lambda j: fg_copy(me, j).wait_send())
    others(lambda j: mp_copy(me, j).wait_send())
    span(0, me, lambda j: d_copy(me, j).wait_send())
    span(me + 1, n, lambda j: u_copy(me, j).wait_send())

    @pl.when(me < n - 1)
    def _():
        rim_copy(me + 1).wait_send()

    @pl.when(me > 0)
    def _():
        dv_copy(me - 1).wait_send()


def store(*refs):
    count = (len(refs) - 1) // 2
    gives = [pltpu.make_async_copy(refs[i], refs[count + i], refs[-1].at[i]) for i in range(count)]
    for give in gives:
        give.start()
    for give in gives:
        give.wait()


def local(x, og, ig, oc, filt, res, rate):
    n = lax.axis_size(AXIS)
    rows, chans = x.shape
    modes, own = rate.shape
    groups = filt.shape[1]
    assert rows == filt.shape[0] and modes & (modes - 1) == 0 and 2 * (modes // 8) * own <= 128 and modes % 8 == 0
    fwd, inv = dft_tables(rows)
    hbm = pl.BlockSpec(memory_space=pltpu.HBM)
    vmem = pl.BlockSpec(memory_space=pltpu.VMEM)
    wide = (rows, chans)
    dma = pltpu.SemaphoreType.DMA
    out = pl.pallas_call(
        functools.partial(kernel, n),
        name="mixer",
        out_shape=(
            pltpu.VMEM(wide, BF16),
            pltpu.VMEM(wide, BF16),
            pltpu.VMEM(wide, BF16),
            pltpu.VMEM((groups, rows), F32),
            pltpu.VMEM((modes, own), F32),
            pltpu.VMEM((modes, own), F32),
        ),
        in_specs=[hbm] * 9,
        out_specs=(vmem,) * 6,
        scratch_shapes=[
            pltpu.VMEM(wide, BF16),
            pltpu.VMEM((n, 8, 128), F32),
            pltpu.VMEM((n, modes, chans), BF16),
            pltpu.VMEM((n, modes, chans), BF16),
            pltpu.VMEM(wide, BF16),
            pltpu.VMEM(wide, BF16),
            pltpu.VMEM((n, 8, 128), F32),
            pltpu.VMEM((n, 8, 128), F32),
            pltpu.VMEM((n, groups, rows), BF16),
            pltpu.VMEM((modes, chans), F32),
            pltpu.VMEM((modes, chans), F32),
            pltpu.VMEM((modes,) + wide, F32),
            pltpu.VMEM((modes,) + wide, F32),
            pltpu.VMEM((modes, chans), F32),
            pltpu.VMEM(wide, F32),
            pltpu.VMEM((2 * modes, chans), F32),
            pltpu.VMEM((2 * modes, chans), F32),
            pltpu.VMEM((2 * modes, chans), F32),
            pltpu.VMEM(wide, F32),
            pltpu.VMEM(wide, F32),
            pltpu.VMEM(wide, F32),
            pltpu.VMEM(wide, F32),
            pltpu.VMEM(wide, F32),
            pltpu.VMEM((2 * rows, chans), F32),
            pltpu.VMEM((2 * rows, chans), F32),
            pltpu.VMEM(wide, BF16),
            pltpu.VMEM(wide, BF16), pltpu.VMEM(wide, BF16), pltpu.VMEM(wide, BF16), pltpu.VMEM(wide, BF16),
            pltpu.VMEM((groups, rows), BF16), pltpu.VMEM((modes, own), F32), pltpu.VMEM((modes, own), F32),
            pltpu.VMEM(fwd.shape, BF16), pltpu.VMEM(inv.shape, BF16), dma((9,)),
            dma((2,)), dma((n,)), dma((n,)), dma((n,)), dma((n,)), dma((n,)), dma((n,)), dma((2,)),
            dma((n,)), dma((n,)), dma((n,)), dma((n,)),
        ],
        compiler_params=pltpu.CompilerParams(
            collective_id=0, has_side_effects=True, vmem_limit_bytes=GRANT
        ),
    )(x, og, ig, oc, filt.T, res, rate, jnp.asarray(fwd), jnp.asarray(inv))
    xg, ogg, igg, fg, rg, tg = pl.pallas_call(
        store,
        name="store",
        out_shape=tuple(jax.ShapeDtypeStruct(o.shape, o.dtype) for o in out),
        in_specs=[vmem] * 6,
        out_specs=(hbm,) * 6,
        scratch_shapes=[dma((6,))],
        compiler_params=pltpu.CompilerParams(vmem_limit_bytes=GRANT),
    )(*[pltpu.with_memory_space_constraint(o, pltpu.VMEM) for o in out])
    return xg, ogg, igg, fg.T, rg, tg


def solution(mesh):
    tokens = P("ctx", "ch")
    shared = P(None, "ch")
    owned = P(None, ("ch", "ctx"))
    return jax.shard_map(
        local,
        mesh=mesh,
        in_specs=(tokens, tokens, tokens, tokens, shared, owned, owned),
        out_specs=(tokens, tokens, tokens, shared, owned, owned),
        check_vma=False,
    )
```

profile of v0, /device:TPU:0, one launch (start us, length us, event | category | flops | bytes accessed | tf_op | source)
XLA Modules:
  0.0 21.4 jit_solution(2522656829919844368)
XLA Ops:
  0.6 20.1 %mixer.1 = (bf16[128,256]{1,0:T(8,128)(2,1)S(1)}, bf16[128,256]{1,0:T(8,128)(2,1)S(1)}, bf16[128,256]{1,0:T(8,128)(2,1)S(1)}, f32[16,128]{1,0:T(8,128)S(1)}, f32[16,32]{1,0:T(8,128)S(1)}, /*index=5*/f32[16,32]{1,0:T(8,128)S(1)}) custom-call(bf16[128,256]{1,0:T(8,128)(2,1)} %x_hbm.1, bf16[128,256]{1,0:T(8,128)(2,1)} %og_hbm.1, bf16[128,256]{1,0:T(8,128)(2,1)} %ig_hbm.1, ...), custom_call_target="tpu_custom_call" | custom-call | tf_op jit(solution)/shard_map/mixer/pallas_call | solution.py:390
  20.7 0.7 %store.1 = (bf16[128,256]{1,0:T(8,128)(2,1)}, bf16[128,256]{1,0:T(8,128)(2,1)}, bf16[128,256]{1,0:T(8,128)(2,1)}, f32[16,128]{1,0:T(8,128)}, f32[16,32]{1,0:T(8,128)}, /*index=5*/f32[16,32]{1,0:T(8,128)}) custom-call(bf16[128,256]{1,0:T(8,128)(2,1)S(1)} %get-tuple-element.18.refs_0_, bf16[128,256]{1,0:T(8,128)(2,1)S(1)} %get-tuple-element.19.refs_1_, ...), custom_call_target="tpu_custom_call" | custom-call | tf_op jit(solution)/shard_map/store/pallas_call | solution.py:440
where the time goes:
time: 21.7 us; the launch traced here: 21.4 us
  Pallas kernels  20.8 us (96%)
  between operations  0.64 us (3%)
    pallas_call x1, Pallas kernels, local(): pl.pallas_call(functools.partial(kernel, n), name='mixer', out_shape=(plt...  20.1 us
    pallas_call x1, Pallas kernels, local(): pl.pallas_call(store, name='store', out_shape=tuple((jax.ShapeDtypeStruct...  0.73 us

commit v1 on v0

v1 whole, which is shorter than its diff:
```python
import functools
import math

import jax
import jax.numpy as jnp
import numpy as np
from jax import lax
from jax.experimental import pallas as pl
from jax.experimental.pallas import tpu as pltpu
from jax.sharding import PartitionSpec as P

MESH = pl.DeviceIdType.MESH
F32, BF16 = jnp.float32, jnp.bfloat16
AXIS = "ctx"
GRANT = 60 * 1024 * 1024
RATE_MAX = 0.03


def pair(table):
    table = table.astype(np.float32)
    high = table.astype(BF16)
    return high, (table - high.astype(np.float32)).astype(BF16)


def dft_tables(half):
    size = 2 * half
    k = np.arange(half)[:, None]
    t = np.arange(half)[None, :]
    angle = 2.0 * np.pi * (k * t % size) / size
    real, imag = np.cos(angle), -np.sin(angle)
    imag[0] = np.cos(np.pi * np.arange(half))
    forward = np.concatenate([real, imag], axis=0)
    gain = np.full((size, 1), 2.0 / size)
    gain[0] = gain[half] = 1.0 / size
    inverse = (forward * gain).T
    return (
        np.concatenate(pair(forward), axis=1),
        np.concatenate(pair(inverse), axis=0),
        np.concatenate(pair(inverse.T), axis=1),
    )


def basis(rows):
    t = np.arange(rows)
    probe = np.linspace(0.0, RATE_MAX, 97)[None, :]
    count = 4
    while True:
        j = np.arange(count)
        node = (rows - 1) / 2 * (1.0 - np.cos((2 * j + 1) * np.pi / (2 * count)))
        base = np.ones((rows, count))
        for a in range(count):
            for b in range(count):
                if a != b:
                    base[:, a] *= (t - node[b]) / (node[a] - node[b])
        error = np.abs(base @ np.exp(-probe * node[:, None]) - np.exp(-probe * t[:, None])).max()
        if error < 2.0**-26:
            return node, base
        count += 2


def node_tables(rows):
    node, base = basis(rows)
    count = len(node)
    pad = -count % 16
    moment = np.pad(base.T, ((0, pad), (0, 0)))
    turned = np.pad(base[::-1].T, ((0, pad), (0, 0)))
    lag = np.arange(rows)[:, None] - np.arange(rows)[None, :]
    lower = np.where((lag >= 0)[None], base.T[:, np.abs(lag)], 0.0)
    upper = np.swapaxes(lower, 1, 2)
    wide = np.repeat(np.stack([base, base[::-1]]), 8, axis=2)
    high, low = pair(wide)
    return (
        node,
        np.concatenate(pair(np.concatenate([moment, turned])), axis=1),
        np.concatenate(pair(upper.reshape(count * rows, rows)), axis=1),
        np.concatenate(pair(lower.reshape(count * rows, rows)), axis=1),
        np.concatenate([high, low, high], axis=2),
    )


def dot(left, right):
    return jnp.dot(left, right, preferred_element_type=F32)


def split(value):
    high = value.astype(BF16)
    return high, (value - high.astype(F32)).astype(BF16)


def product(left, right):
    return (left.astype(F32) * right.astype(F32)).astype(BF16)


def twice(value):
    return jnp.concatenate([value, value], axis=0)


def kernel(
    n, node, x_hbm, og_hbm, ig_hbm, oc_hbm, filt_hbm, res_hbm, rate_hbm, dft_hbm, mom_hbm, far_hbm, up_hbm, lo_hbm,
    xg_ref, ogg_ref, igg_ref, fg_ref, rg_ref, tg_ref,
    rim, rr_send, rr_all, du_send, du_all, dv, dv_rim, p_send, p_all, fg_send, fg_all,
    rates, resid, e_ref, h_ref, b_ref, row_ref, far_ref, pb_ref, g_ref,
    back_ref, conv_ref, xs_ref, fs_ref, mr_ref,
    wide_ref, filt_ref, own_ref, dft_ref, mom_ref, ft_ref, up_ref, lo_ref, in_sem,
    rim_sem, dv_sem, all_sem, du_recv,
):
    me = lax.axis_index(AXIS)
    barrier = pltpu.get_barrier_semaphore()

    def others(act):
        def step(k, carry):
            act(lax.rem(me + k, n))
            return carry

        lax.fori_loop(1, n, step, 0)

    def span(lo, hi, act):
        def step(j, carry):
            act(j)
            return carry

        lax.fori_loop(lo, hi, step, 0)

    others(lambda j: pl.semaphore_signal(barrier, inc=1, device_id={AXIS: j}, device_id_type=MESH))

    def load(src, dst, i):
        return pltpu.make_async_copy(src, dst, in_sem.at[i])

    load(rate_hbm, own_ref.at[0], 0).start()
    load(res_hbm, own_ref.at[1], 0).start()
    load(og_hbm, wide_ref.at[0], 1).start()
    load(oc_hbm, wide_ref.at[1], 1).start()
    load(mom_hbm, mom_ref, 2).start()
    load(up_hbm, up_ref, 3).start()
    load(x_hbm, wide_ref.at[2], 4).start()
    load(ig_hbm, wide_ref.at[3], 4).start()
    load(filt_hbm, filt_ref, 5).start()
    load(dft_hbm, dft_ref, 6).start()
    load(far_hbm, ft_ref, 7).start()
    load(lo_hbm, lo_ref, 8).start()
    og_ref, oc_ref, x_ref, ig_ref = (wide_ref.at[i] for i in range(4))
    rate_ref, res_ref = own_ref.at[0], own_ref.at[1]

    rows, chans = x_hbm.shape
    modes, own = rate_hbm.shape
    groups = filt_hbm.shape[0]
    parts = modes // 8
    count = len(node)
    tall = mom_ref.shape[0] // 2

    def remote(src, dst, ssem, rsem, to):
        return pltpu.make_async_remote_copy(
            src_ref=src, dst_ref=dst, send_sem=ssem, recv_sem=rsem, device_id={AXIS: to}, device_id_type=MESH
        )

    def rr_copy(to):
        return remote(rr_send, rr_all.at[me], all_sem.at[0], all_sem.at[1], to)

    def p_copy(to):
        return remote(p_send.at[to], p_all.at[me], all_sem.at[2], all_sem.at[3], to)

    def fg_copy(to):
        return remote(fg_send, fg_all.at[me], all_sem.at[4], all_sem.at[5], to)

    def du_copy(which, slot, to):
        return remote(du_send.at[which], du_all.at[slot], all_sem.at[6], du_recv.at[slot], to)

    def rim_copy(to):
        return remote(x_ref, rim, rim_sem.at[0], rim_sem.at[1], to)

    def dv_copy(to):
        return remote(dv, dv_rim, dv_sem.at[0], dv_sem.at[1], to)

    def take(ref, i):
        part = ref.at[pl.ds(0, n - 1)]
        pltpu.make_async_copy(part, part, all_sem.at[i]).wait()

    p_send[...] = jnp.zeros_like(p_send)
    g_ref[...] = jnp.zeros_like(g_ref)
    load(own_ref, own_ref, 0).wait()
    for g in range(parts):
        rr_send[:, g * own : (g + 1) * own] = rate_ref[8 * g : 8 * g + 8, :]
        rr_send[:, (parts + g) * own : (parts + g + 1) * own] = res_ref[8 * g : 8 * g + 8, :]

    load(wide_ref.at[pl.ds(0, 2)], wide_ref.at[pl.ds(0, 2)], 1).wait()
    load(mom_ref, mom_ref, 2).wait()
    dz2 = twice(product(og_ref[...], oc_ref[...]))
    du_send[0] = dot(mom_ref[:tall, :], dz2).astype(BF16)
    load(up_ref, up_ref, 3).wait()
    for j in range(count):
        b_ref[j] = dot(up_ref[j * rows : (j + 1) * rows, :], dz2)

    load(wide_ref.at[pl.ds(2, 2)], wide_ref.at[pl.ds(2, 2)], 4).wait()
    load(filt_hbm, filt_ref, 5).wait()
    load(dft_hbm, dft_ref, 6).wait()
    load(far_hbm, ft_ref, 7).wait()
    fwd = dft_ref[0]
    inv_hi = dft_ref[1, :rows, :]
    inv_lo = dft_ref[1, rows:, :]
    first_row = lax.broadcasted_iota(jnp.int32, (rows, chans), 0) == 0
    sign = (1 - 2 * lax.rem(lax.broadcasted_iota(jnp.int32, (2 * rows, chans), 0), 2)).astype(F32)

    def spectrum(value):
        return dot(fwd, twice(value))

    def signal(spec):
        high, low = split(spec)
        return dot(inv_hi, high) + dot(inv_hi, low) + dot(inv_lo, high)

    def times(a, b, conj):
        ar, ai, br, bi = a[:rows], a[rows:], b[:rows], b[rows:]
        pure = ai * bi
        cross = jnp.where(first_row, 0.0, pure)
        if conj:
            return jnp.concatenate([ar * br + cross, jnp.where(first_row, pure, ar * bi - ai * br)], axis=0)
        return jnp.concatenate([ar * br - cross, jnp.where(first_row, pure, ar * bi + ai * br)], axis=0)

    member = (
        lax.broadcasted_iota(jnp.int32, (groups, chans), 1) // (chans // groups)
        == lax.broadcasted_iota(jnp.int32, (groups, chans), 0)
    ).astype(BF16)
    taps = lax.dot_general(
        filt_ref[...], member, (((0,), (0,)), ((), ())), preferred_element_type=F32
    ).astype(BF16)
    fs_ref[...] = spectrum(taps)
    xs_ref[...] = spectrum(x_ref[...])

    pl.semaphore_wait(barrier, n - 1)
    others(lambda j: rr_copy(j).start())
    span(0, me, lambda j: du_copy(0, me, j).start())

    @pl.when(me < n - 1)
    def _():
        rim_copy(me + 1).start()

    rr_all[me] = rr_send[...]

    @pl.when(me == 0)
    def _():
        rim[...] = jnp.zeros_like(rim)

    @pl.when(me > 0)
    def _():
        rim_copy(me).wait_recv()

    xs = xs_ref[...] + sign * spectrum(rim[...])
    xs_ref[...] = xs
    mr = signal(times(fs_ref[...], xs, False)).astype(BF16)
    mr_ref[...] = mr
    u = product(ig_ref[...], mr)
    u2 = twice(u)
    state = dot(mom_ref[tall:, :], u2).astype(BF16)
    du_send[1] = state
    span(me + 1, n, lambda j: du_copy(1, me, j).start())
    for j in range(count):
        total = jnp.zeros((8, chans), F32)
        for t in range(rows // 8):
            total += b_ref[j, 8 * t : 8 * t + 8, :] * u[8 * t : 8 * t + 8, :].astype(F32)
        g_ref[j : j + 1, :] = jnp.sum(total, axis=0, keepdims=True)
    lag = g_ref[...].astype(BF16)
    here = du_send[0]
    for j in range(n):
        at = slice(j * own, (j + 1) * own)
        p_send[j, :, :own] = state[:, at]
        p_send[j, :, own : 2 * own] = here[:, at]
        p_send[j, :, 2 * own : 3 * own] = lag[:, at]
    p_all[me] = p_send[me]
    others(lambda j: p_copy(j).start())

    take(rr_all, 1)
    for j in range(n):
        piece = rr_all[j]
        for g in range(parts):
            rates[8 * g : 8 * g + 8, j * own : (j + 1) * own] = piece[:, g * own : (g + 1) * own]
            resid[8 * g : 8 * g + 8, j * own : (j + 1) * own] = piece[:, (parts + g) * own : (parts + g + 1) * own]
    rate = rates[...]
    weight = resid[...] * jnp.sqrt(2.0 * rate / modes)
    resid[...] = weight
    for j in range(count):
        e = jnp.exp(-float(node[j]) * rate)
        e_ref[j] = e
        h_ref[j : j + 1, :] = jnp.sum(weight * e, axis=0, keepdims=True)

    def jump():
        return jnp.exp(-rates[...] * rows)

    def gather(slot, carry):
        row_ref[...] = du_all[slot].astype(F32)
        for j in range(count):
            carry += e_ref[j] * row_ref[j : j + 1, :]
        return carry

    def spread(state, which):
        coef = resid[...] * jnp.exp(-rates[...]) * state
        for j in range(count):
            part = coef * e_ref[j]
            total = part[:8]
            for g in range(1, parts):
                total += part[8 * g : 8 * g + 8]
            pb_ref[8 * j : 8 * j + 8, :] = total
        high, low = split(pb_ref[...])
        far_ref[...] = dot(ft_ref[which], jnp.concatenate([high, high, low], axis=0))

    @pl.when(me == n - 1)
    def _():
        far_ref[...] = jnp.zeros_like(far_ref)

    @pl.when(me < n - 1)
    def _():
        span(me + 1, n, lambda j: du_copy(0, j, j).wait_recv())
        decay = jump()
        spread(
            lax.fori_loop(0, n - 1 - me, lambda i, q: gather(n - 1 - i, q * decay), jnp.zeros((modes, chans), F32)), 1
        )

    def blocks(act):
        step = 32

        def body(i, carry):
            act(pl.ds(pl.multiple_of(step * i, step), step))
            return carry

        lax.fori_loop(0, rows // step, body, 0)

    def gates(at):
        total = far_ref[at, :]
        for j in range(count):
            total += h_ref[j : j + 1, :] * b_ref[j, at, :]
        back = total.astype(BF16)
        dv[at, :] = product(back, ig_ref[at, :])
        igg_ref[at, :] = product(back, mr_ref[at, :])

    blocks(gates)

    @pl.when(me > 0)
    def _():
        dv_copy(me - 1).start()

    dvs = spectrum(dv[...])
    c_hi, c_lo = split(times(xs_ref[...], dvs, True))
    nt = (((1,), (1,)), ((), ()))
    sums = lax.dot_general(member, c_hi, nt, preferred_element_type=F32) + lax.dot_general(
        member, c_lo, nt, preferred_element_type=F32
    )
    both = dot(jnp.concatenate(split(sums), axis=0), dft_ref[2])
    fg_send[...] = (both[:groups, :rows] + both[groups:, :rows] + both[:groups, rows:]).astype(BF16)
    others(lambda j: fg_copy(j).start())
    fg_all[me] = fg_send[...]

    load(lo_hbm, lo_ref, 8).wait()
    conv = jnp.zeros((rows, chans), F32)
    for j in range(count):
        conv += h_ref[j : j + 1, :] * dot(lo_ref[j * rows : (j + 1) * rows, :], u2)
    conv_ref[...] = conv

    @pl.when(me == 0)
    def _():
        far_ref[...] = jnp.zeros_like(far_ref)

    @pl.when(me > 0)
    def _():
        span(0, me, lambda j: du_copy(1, j, j).wait_recv())
        decay = jump()
        spread(lax.fori_loop(0, me, lambda i, s: gather(i, s * decay), jnp.zeros((modes, chans), F32)), 0)

    conv = (conv_ref[...] + far_ref[...]).astype(BF16)
    ogg_ref[...] = product(oc_ref[...], conv)

    take(p_all, 3)
    scale = 1.0 / math.sqrt(rows * n)
    lanes = p_all.shape[2]
    mine = rate_ref[...]
    fold = jnp.concatenate([mine] * (lanes // own), axis=1)
    hop = jnp.exp(-float(rows) * fold)

    def owner(b, carry):
        s, far, first, second, near0, near1 = carry
        row_ref[:, :lanes] = p_all[b].astype(F32)
        zero = one = jnp.zeros((modes, lanes), F32)
        for j in range(count):
            part = jnp.exp(-float(node[j]) * fold) * row_ref[j : j + 1, :lanes]
            zero += part
            one += float(node[j]) * part
        d0 = pltpu.roll(zero, lanes - own, 1)
        d1 = pltpu.roll(one, lanes - own, 1)
        first += d0 * s
        second += (d0 + d1) * s + d0 * far
        return s * hop + zero, (far + rows * s) * hop + one, first, second, near0 + zero, near1 + one

    empty = jnp.zeros((modes, lanes), F32)
    _, _, first, second, near0, near1 = lax.fori_loop(0, n, owner, (empty,) * 6)
    step = jnp.exp(-fold)
    first = (step * first + pltpu.roll(near0, lanes - 2 * own, 1))[:, :own]
    second = (step * second + pltpu.roll(near1, lanes - 2 * own, 1))[:, :own]
    gain = jnp.sqrt(2.0 * mine / modes)
    rg_ref[...] = gain * first * scale
    tg_ref[...] = res_ref[...] * gain * (0.5 * first - mine * second) * scale

    @pl.when(me == n - 1)
    def _():
        dv_rim[...] = jnp.zeros_like(dv_rim)

    @pl.when(me < n - 1)
    def _():
        dv_copy(me).wait_recv()

    ws = dvs + sign * spectrum(dv_rim[...])
    xg_ref[...] = signal(times(fs_ref[...], ws, True)).astype(BF16)

    take(rr_all, 0)
    take(p_all, 2)
    take(du_all, 6)

    @pl.when(me < n - 1)
    def _():
        rim_copy(me + 1).wait_send()

    @pl.when(me > 0)
    def _():
        dv_copy(me - 1).wait_send()

    take(fg_all, 4)
    take(fg_all, 5)
    fg_ref[...] = jnp.sum(fg_all[...].astype(F32), axis=0) * scale


def store(*refs):
    count = (len(refs) - 1) // 2
    gives = [pltpu.make_async_copy(refs[i], refs[count + i], refs[-1].at[i]) for i in range(count)]
    for give in gives:
        give.start()
    for give in gives:
        give.wait()


def local(x, og, ig, oc, filt, res, rate):
    n = lax.axis_size(AXIS)
    rows, chans = x.shape
    modes, own = rate.shape
    groups = filt.shape[1]
    assert rows == filt.shape[0] and modes % 8 == 0 and 2 * (modes // 8) * own <= 128 and 128 % own == 0
    fwd, inv, turn = dft_tables(rows)
    node, mom, up, lo, far = node_tables(rows)
    count = len(node)
    tall = mom.shape[0] // 2
    hbm = pl.BlockSpec(memory_space=pltpu.HBM)
    vmem = pl.BlockSpec(memory_space=pltpu.VMEM)
    wide = (rows, chans)
    dma = pltpu.SemaphoreType.DMA
    out = pl.pallas_call(
        functools.partial(kernel, n, tuple(float(v) for v in node)),
        name="mixer",
        out_shape=(
            pltpu.VMEM(wide, BF16),
            pltpu.VMEM(wide, BF16),
            pltpu.VMEM(wide, BF16),
            pltpu.VMEM((groups, rows), F32),
            pltpu.VMEM((modes, own), F32),
            pltpu.VMEM((modes, own), F32),
        ),
        in_specs=[hbm] * 12,
        out_specs=(vmem,) * 6,
        scratch_shapes=[
            pltpu.VMEM(wide, BF16),
            pltpu.VMEM((8, 128), F32),
            pltpu.VMEM((n, 8, 128), F32),
            pltpu.VMEM((2, tall, chans), BF16),
            pltpu.VMEM((n, tall, chans), BF16),
            pltpu.VMEM(wide, BF16),
            pltpu.VMEM(wide, BF16),
            pltpu.VMEM((n, tall, 128), BF16),
            pltpu.VMEM((n, tall, 128), BF16),
            pltpu.VMEM((groups, rows), BF16),
            pltpu.VMEM((n, groups, rows), BF16),
            pltpu.VMEM((modes, chans), F32),
            pltpu.VMEM((modes, chans), F32),
            pltpu.VMEM((count, modes, chans), F32),
            pltpu.VMEM((tall, chans), F32),
            pltpu.VMEM((count,) + wide, F32),
            pltpu.VMEM((tall, chans), F32),
            pltpu.VMEM(wide, F32),
            pltpu.VMEM((8 * count, chans), F32),
            pltpu.VMEM((tall, chans), F32),
            pltpu.VMEM(wide, F32),
            pltpu.VMEM(wide, F32),
            pltpu.VMEM((2 * rows, chans), F32),
            pltpu.VMEM((2 * rows, chans), F32),
            pltpu.VMEM(wide, BF16),
            pltpu.VMEM((4,) + wide, BF16),
            pltpu.VMEM((groups, rows), BF16),
            pltpu.VMEM((2, modes, own), F32),
            pltpu.VMEM((3, 2 * rows, 2 * rows), BF16),
            pltpu.VMEM(mom.shape, BF16),
            pltpu.VMEM(far.shape, BF16),
            pltpu.VMEM(up.shape, BF16),
            pltpu.VMEM(lo.shape, BF16),
            dma((9,)),
            dma((2,)), dma((2,)), dma((7,)), dma((n,)),
        ],
        compiler_params=pltpu.CompilerParams(
            collective_id=0, has_side_effects=True, vmem_limit_bytes=GRANT
        ),
    )(
        x, og, ig, oc, filt.T, res, rate,
        jnp.asarray(np.stack([fwd, inv, turn])), jnp.asarray(mom), jnp.asarray(far), jnp.asarray(up), jnp.asarray(lo),
    )
    xg, ogg, igg, fg, rg, tg = pl.pallas_call(
        store,
        name="store",
        out_shape=tuple(jax.ShapeDtypeStruct(o.shape, o.dtype) for o in out),
        in_specs=[vmem] * 6,
        out_specs=(hbm,) * 6,
        scratch_shapes=[dma((6,))],
        compiler_params=pltpu.CompilerParams(vmem_limit_bytes=GRANT),
    )(*[pltpu.with_memory_space_constraint(o, pltpu.VMEM) for o in out])
    return xg, ogg, igg, fg.T, rg, tg


def solution(mesh):
    tokens = P("ctx", "ch")
    shared = P(None, "ch")
    owned = P(None, ("ch", "ctx"))
    return jax.shard_map(
        local,
        mesh=mesh,
        in_specs=(tokens, tokens, tokens, tokens, shared, owned, owned),
        out_specs=(tokens, tokens, tokens, shared, owned, owned),
        check_vma=False,
    )
```

time: 21.7 us -> 17.2 us (0.79)
  Pallas kernels: 20.8 us -> 16.3 us
    pallas_call x1, Pallas kernels: 20.1 us -> 15.6 us  [local(): pl.pallas_call(functools.partial(kernel, n, tuple((float(v) for v in node...]
where the time goes in v1:
time: 17.2 us; the launch traced here: 17 us
  Pallas kernels  16.3 us (95%)
  between operations  0.64 us (4%)
    pallas_call x1, Pallas kernels, local(): pl.pallas_call(functools.partial(kernel, n, tuple((float(v) for v in node...  15.6 us
    pallas_call x1, Pallas kernels, local(): pl.pallas_call(store, name='store', out_shape=tuple((jax.ShapeDtypeStruct...  0.73 us

profile of v1, /device:TPU:0, one launch (start us, length us, event | category | flops | bytes accessed | tf_op | source)
XLA Modules:
  0.0 17.0 jit_solution(1069127328480933515)
XLA Ops:
  0.6 15.6 %mixer.1 = (bf16[128,256]{1,0:T(8,128)(2,1)S(1)}, bf16[128,256]{1,0:T(8,128)(2,1)S(1)}, bf16[128,256]{1,0:T(8,128)(2,1)S(1)}, f32[16,128]{1,0:T(8,128)S(1)}, f32[16,32]{1,0:T(8,128)S(1)}, /*index=5*/f32[16,32]{1,0:T(8,128)S(1)}) custom-call(bf16[128,256]{1,0:T(8,128)(2,1)} %x_hbm.1, bf16[128,256]{1,0:T(8,128)(2,1)} %og_hbm.1, bf16[128,256]{1,0:T(8,128)(2,1)} %ig_hbm.1, ...), custom_call_target="tpu_custom_call" | custom-call | tf_op jit(solution)/shard_map/mixer/pallas_call | solution.py:450
  16.2 0.7 %store.1 = (bf16[128,256]{1,0:T(8,128)(2,1)}, bf16[128,256]{1,0:T(8,128)(2,1)}, bf16[128,256]{1,0:T(8,128)(2,1)}, f32[16,128]{1,0:T(8,128)}, f32[16,32]{1,0:T(8,128)}, /*index=5*/f32[16,32]{1,0:T(8,128)}) custom-call(bf16[128,256]{1,0:T(8,128)(2,1)S(1)} %get-tuple-element.18.refs_0_, bf16[128,256]{1,0:T(8,128)(2,1)S(1)} %get-tuple-element.19.refs_1_, ...), custom_call_target="tpu_custom_call" | custom-call | tf_op jit(solution)/shard_map/store/pallas_call | solution.py:507

commit v2 on v1

v2 whole, which is shorter than its diff:
```python
import functools
import math

import jax
import jax.numpy as jnp
import numpy as np
from jax import lax
from jax.experimental import pallas as pl
from jax.experimental.pallas import tpu as pltpu
from jax.sharding import PartitionSpec as P

MESH = pl.DeviceIdType.MESH
F32, BF16 = jnp.float32, jnp.bfloat16
AXIS = "ctx"
GRANT = 60 * 1024 * 1024
RATE_MAX = 0.03


def pair(table):
    table = table.astype(np.float32)
    high = table.astype(BF16)
    return high, (table - high.astype(np.float32)).astype(BF16)


def dft_tables(half):
    size = 2 * half
    k = np.arange(half)[:, None]
    t = np.arange(half)[None, :]
    angle = 2.0 * np.pi * (k * t % size) / size
    real, imag = np.cos(angle), -np.sin(angle)
    imag[0] = np.cos(np.pi * np.arange(half))
    forward = np.concatenate([real, imag], axis=0)
    gain = np.full((size, 1), 2.0 / size)
    gain[0] = gain[half] = 1.0 / size
    inverse = (forward * gain).T
    return (
        np.concatenate(pair(forward), axis=1),
        np.concatenate(pair(inverse), axis=0),
        np.concatenate(pair(inverse.T), axis=1),
    )


def basis(rows):
    t = np.arange(rows)
    probe = np.linspace(0.0, RATE_MAX, 97)[None, :]
    count = 4
    while True:
        j = np.arange(count)
        node = (rows - 1) / 2 * (1.0 - np.cos((2 * j + 1) * np.pi / (2 * count)))
        base = np.ones((rows, count))
        for a in range(count):
            for b in range(count):
                if a != b:
                    base[:, a] *= (t - node[b]) / (node[a] - node[b])
        error = np.abs(base @ np.exp(-probe * node[:, None]) - np.exp(-probe * t[:, None])).max()
        if error < 2.0**-23:
            return node, base
        count += 2


def node_tables(rows):
    node, base = basis(rows)
    count = len(node)
    pad = -count % 16
    moment = np.pad(base.T, ((0, pad), (0, 0)))
    turned = np.pad(base[::-1].T, ((0, pad), (0, 0)))
    lag = np.arange(rows)[:, None] - np.arange(rows)[None, :]
    lower = np.where((lag >= 0)[None], base.T[:, np.abs(lag)], 0.0)
    upper = np.swapaxes(lower, 1, 2)
    wide = np.repeat(np.concatenate([base, base[::-1]]), 8, axis=1)
    high, low = pair(wide)
    far = np.concatenate([high, high * 0, high * 0], axis=1)
    far[:, 8 * count : 16 * count], far[:, 16 * count :] = low, high
    far = np.pad(far, ((0, 0), (0, 2 * rows - far.shape[1])))
    return (
        node,
        np.concatenate(pair(np.concatenate([moment, turned])), axis=1),
        np.concatenate(pair(upper.reshape(count * rows, rows)), axis=1),
        np.concatenate(pair(lower.reshape(count * rows, rows)), axis=1),
        far,
    )


def dot(left, right):
    return jnp.dot(left, right, preferred_element_type=F32)


def split(value):
    high = value.astype(BF16)
    return high, (value - high.astype(F32)).astype(BF16)


def product(left, right):
    return (left.astype(F32) * right.astype(F32)).astype(BF16)


def twice(value):
    return jnp.concatenate([value, value], axis=0)


def kernel(
    n, node, x_hbm, og_hbm, ig_hbm, oc_hbm, filt_hbm, res_hbm, rate_hbm, mom_hbm, tab_hbm, lo_hbm,
    xg_ref, ogg_ref, igg_ref, fg_ref, rg_ref, tg_ref,
    rim, rr_send, rr_all, du_send, du_all, dv, dv_rim, p_send, p_all, fg_send, fg_all,
    rates, resid, fold_ref, pf_ref, e_ref, h_ref, b_ref, row_ref, far_ref, pb_ref, g_ref,
    conv_ref, xs_ref, fs_ref, ds_ref, mr_ref, u_ref, back_ref,
    wide_ref, filt_ref, own_ref, mom_ref, tab_ref, lo_ref, unit_ref, in_sem,
    rim_sem, dv_sem, all_sem, du_recv,
):
    me = lax.axis_index(AXIS)
    barrier = pltpu.get_barrier_semaphore()

    def others(act):
        def step(k, carry):
            act(lax.rem(me + k, n))
            return carry

        lax.fori_loop(1, n, step, 0)

    def span(lo, hi, act):
        def step(j, carry):
            act(j)
            return carry

        lax.fori_loop(lo, hi, step, 0)

    others(lambda j: pl.semaphore_signal(barrier, inc=1, device_id={AXIS: j}, device_id_type=MESH))

    def load(src, dst, i):
        return pltpu.make_async_copy(src, dst, in_sem.at[i])

    load(rate_hbm, own_ref.at[0], 0).start()
    load(res_hbm, own_ref.at[1], 0).start()
    load(og_hbm, wide_ref.at[0], 1).start()
    load(oc_hbm, wide_ref.at[1], 1).start()
    load(mom_hbm, mom_ref, 2).start()
    load(tab_hbm, tab_ref, 3).start()
    load(x_hbm, wide_ref.at[2], 4).start()
    load(ig_hbm, wide_ref.at[3], 4).start()
    load(filt_hbm, filt_ref, 5).start()
    load(lo_hbm, lo_ref, 6).start()
    og_ref, oc_ref, x_ref, ig_ref = (wide_ref.at[i] for i in range(4))
    rate_ref, res_ref = own_ref.at[0], own_ref.at[1]

    rows, chans = x_hbm.shape
    modes, own = rate_hbm.shape
    groups = filt_hbm.shape[0]
    parts = modes // 8
    count = len(node)
    tall = mom_ref.shape[0] // 2
    size = 2 * rows
    sides = chans // 128
    crowd = n // sides

    def remote(src, dst, ssem, rsem, to):
        return pltpu.make_async_remote_copy(
            src_ref=src, dst_ref=dst, send_sem=ssem, recv_sem=rsem, device_id={AXIS: to}, device_id_type=MESH
        )

    def rr_copy(to):
        return remote(rr_send, rr_all.at[me], all_sem.at[0], all_sem.at[3 + me // crowd], to)

    def p_copy(to):
        return remote(p_send.at[to], p_all.at[me], all_sem.at[0], all_sem.at[1], to)

    def fg_copy(side, to):
        return remote(fg_send.at[side], fg_all.at[me, side], all_sem.at[0], all_sem.at[2], to)

    def du_copy(which, slot, to):
        return remote(du_send.at[which], du_all.at[slot], all_sem.at[0], du_recv.at[slot], to)

    def rim_copy(to):
        return remote(x_ref, rim, rim_sem.at[0], rim_sem.at[1], to)

    def dv_copy(to):
        return remote(dv, dv_rim, dv_sem.at[0], dv_sem.at[1], to)

    def take(ref, i, many):
        part = ref.at[pl.ds(0, many)]
        pltpu.make_async_copy(part, part, all_sem.at[i]).wait()

    p_send[...] = jnp.zeros_like(p_send)
    g_ref[...] = jnp.zeros_like(g_ref)
    load(own_ref, own_ref, 0).wait()
    for g in range(parts):
        rr_send[:, g * own : (g + 1) * own] = rate_ref[8 * g : 8 * g + 8, :]
        rr_send[:, (parts + g) * own : (parts + g + 1) * own] = res_ref[8 * g : 8 * g + 8, :]

    load(wide_ref.at[pl.ds(0, 2)], wide_ref.at[pl.ds(0, 2)], 1).wait()
    load(mom_ref, mom_ref, 2).wait()
    dz2 = twice(product(og_ref[...], oc_ref[...]))
    du_send[0] = dot(mom_ref[:tall, :], dz2).astype(BF16)
    load(wide_ref.at[pl.ds(2, 2)], wide_ref.at[pl.ds(2, 2)], 4).wait()
    pl.semaphore_wait(barrier, n - 1)
    others(lambda j: rr_copy(j).start())
    span(0, me, lambda j: du_copy(0, me, j).start())

    @pl.when(me < n - 1)
    def _():
        rim_copy(me + 1).start()

    rr_all[me] = rr_send[...]
    load(tab_hbm, tab_ref, 3).wait()
    far_at = 3 * size
    up_at = far_at + size
    for j in range(count):
        b_ref[j] = dot(tab_ref[up_at + j * rows : up_at + (j + 1) * rows, :], dz2)

    load(filt_hbm, filt_ref, 5).wait()
    fwd = tab_ref[:size, :]
    inv_hi = tab_ref[size : size + rows, :]
    inv_lo = tab_ref[size + rows : 2 * size, :]
    sign = (1 - 2 * lax.rem(lax.broadcasted_iota(jnp.int32, (size, chans), 0), 2)).astype(F32)

    def spectrum(value):
        return dot(fwd, twice(value))

    def signal(spec):
        high, low = split(spec)
        return dot(inv_hi, high) + dot(inv_hi, low) + dot(inv_lo, high)

    def times(a, b, conj):
        ar, ai, br, bi = a[:rows], a[rows:], b[:rows], b[rows:]
        first_row = lax.broadcasted_iota(jnp.int32, ai.shape, 0) == 0
        pure = ai * bi
        cross = jnp.where(first_row, 0.0, pure)
        if conj:
            return jnp.concatenate([ar * br + cross, jnp.where(first_row, pure, ar * bi - ai * br)], axis=0)
        return jnp.concatenate([ar * br - cross, jnp.where(first_row, pure, ar * bi + ai * br)], axis=0)

    member = (
        lax.broadcasted_iota(jnp.int32, (groups, chans), 1) // (chans // groups)
        == lax.broadcasted_iota(jnp.int32, (groups, chans), 0)
    ).astype(BF16)
    taps = lax.dot_general(
        filt_ref[...], member, (((0,), (0,)), ((), ())), preferred_element_type=F32
    ).astype(BF16)
    fs_ref[...] = spectrum(taps)
    xs_ref[...] = spectrum(x_ref[...])

    def mix():
        @pl.when(me == 0)
        def _():
            rim[...] = jnp.zeros_like(rim)

        @pl.when(me > 0)
        def _():
            rim_copy(me).wait_recv()

        xs = xs_ref[...] + sign * spectrum(rim[...])
        xs_ref[...] = xs
        mr = signal(times(fs_ref[...], xs, False)).astype(BF16)
        mr_ref[...] = mr
        u = product(ig_ref[...], mr)
        u_ref[...] = u
        u2 = twice(u)
        state = dot(mom_ref[tall:, :], u2).astype(BF16)
        du_send[1] = state
        span(me + 1, n, lambda j: du_copy(1, me, j).start())
        for j in range(count):
            total = jnp.zeros((8, chans), F32)
            for t in range(rows // 8):
                total += b_ref[j, 8 * t : 8 * t + 8, :] * u[8 * t : 8 * t + 8, :].astype(F32)
            g_ref[j : j + 1, :] = jnp.sum(total, axis=0, keepdims=True)
        lag = g_ref[...].astype(BF16)
        here = du_send[0]
        for j in range(n):
            at = slice(j * own, (j + 1) * own)
            p_send[j, :, :own] = state[:, at]
            p_send[j, :, own : 2 * own] = here[:, at]
            p_send[j, :, 2 * own : 3 * own] = lag[:, at]
        p_all[me] = p_send[me]
        others(lambda j: p_copy(j).start())

    mine = rate_ref[...]
    lanes = p_all.shape[2]
    fold = jnp.concatenate([mine] * (lanes // own), axis=1)
    for j in range(count):
        fold_ref[j] = jnp.exp(-float(node[j]) * fold)

    def gather(slot, carry, cols):
        row_ref[:, cols] = du_all[slot, :, cols].astype(F32)
        for j in range(count):
            carry += e_ref[j, :, cols] * row_ref[j : j + 1, cols]
        return carry

    def spread(state, which, cols):
        coef = resid[:, cols] * jnp.exp(-rates[:, cols]) * state
        for j in range(count):
            part = coef * e_ref[j, :, cols]
            total = part[:8]
            for g in range(1, parts):
                total += part[8 * g : 8 * g + 8]
            pb_ref[8 * j : 8 * j + 8, cols] = total
        high, low = split(pb_ref[:, cols])
        stack = [high, high, low]
        spare = size - 3 * high.shape[0]
        if spare:
            stack.append(jnp.zeros((spare, high.shape[1]), BF16))
        table = tab_ref[far_at + which * rows : far_at + (which + 1) * rows, :]
        far_ref[:, cols] = dot(table, jnp.concatenate(stack, axis=0))

    @pl.when(me == n - 1)
    def _():
        far_ref[...] = jnp.zeros_like(far_ref)

    nt = (((1,), (1,)), ((), ()))
    few = groups // sides
    turn = tab_ref[2 * size : 3 * size, :]
    def grad(side):
        cols = slice(128 * side, 128 * side + 128)

        @pl.when(me // crowd == side)
        def _(side=side):
            take(rr_all, 3 + side, crowd - 1)

        @pl.when(me // crowd != side)
        def _(side=side):
            take(rr_all, 3 + side, crowd)

        for j in range(side * crowd, (side + 1) * crowd):
            piece = rr_all[j]
            for g in range(parts):
                at = (slice(8 * g, 8 * g + 8), slice(j * own, (j + 1) * own))
                rates[at] = piece[:, g * own : (g + 1) * own]
                resid[at] = piece[:, (parts + g) * own : (parts + g + 1) * own]
        rate = rates[:, cols]
        weight = resid[:, cols] * jnp.sqrt(2.0 * rate / modes)
        resid[:, cols] = weight
        for j in range(count):
            e = jnp.exp(-float(node[j]) * rate)
            e_ref[j, :, cols] = e
            h_ref[j : j + 1, cols] = jnp.sum(weight * e, axis=0, keepdims=True)

        @pl.when(me < n - 1)
        def _(side=side, cols=cols):
            if side == sides - 1:
                span(me + 1, n, lambda j: du_copy(0, j, j).wait_recv())
            decay = jnp.exp(-rates[:, cols] * rows)
            start = jnp.zeros((modes, 128), F32)
            spread(
                lax.fori_loop(0, n - 1 - me, lambda i, q: gather(n - 1 - i, q * decay, cols), start), 1, cols
            )

        chunk = 32
        for at in range(0, rows, chunk):
            here = slice(at, at + chunk)
            total = far_ref[here, cols]
            for j in range(count):
                total += h_ref[j : j + 1, cols] * b_ref[j, here, cols]
            back = total.astype(BF16)
            back_ref[here, cols] = back
            dv[here, cols] = product(back, ig_ref[here, cols])

    def tap(side):
        cols = slice(128 * side, 128 * side + 128)
        spec = spectrum(dv[:, cols])
        ds_ref[:, cols] = spec
        cross = times(xs_ref[:, cols], spec, True).astype(BF16)
        sums = lax.dot_general(
            member[side * few : (side + 1) * few, cols], cross, nt, preferred_element_type=F32
        )
        both = dot(jnp.concatenate(split(sums), axis=0), turn)
        fg_send[side] = (both[:few, :rows] + both[few:, :rows] + both[:few, rows:]).astype(BF16)
        others(lambda j: fg_copy(side, j).start())

    def hand():
        @pl.when(me > 0)
        def _():
            dv_copy(me - 1).start()

    @pl.when(me >= n // 2)
    def _():
        mix()
        for side in reversed(range(sides)):
            grad(side)
            if side == 0:
                hand()
            tap(side)

    @pl.when(me < n // 2)
    def _():
        for side in reversed(range(sides)):
            grad(side)
        hand()
        mix()
        for side in reversed(range(sides)):
            tap(side)

    fg_all[me] = fg_send[...]
    igg_ref[...] = product(back_ref[...], mr_ref[...])
    u2 = twice(u_ref[...])

    load(lo_hbm, lo_ref, 6).wait()
    conv = jnp.zeros((rows, chans), F32)
    for j in range(count):
        conv += h_ref[j : j + 1, :] * dot(lo_ref[j * rows : (j + 1) * rows, :], u2)
    conv_ref[...] = conv

    @pl.when(me == 0)
    def _():
        far_ref[...] = jnp.zeros_like(far_ref)

    @pl.when(me > 0)
    def _():
        span(0, me, lambda j: du_copy(1, j, j).wait_recv())
        decay = jnp.exp(-rates[...] * rows)
        every = slice(0, chans)
        start = jnp.zeros((modes, chans), F32)
        spread(lax.fori_loop(0, me, lambda i, s: gather(i, s * decay, every), start), 0, every)

    conv = (conv_ref[...] + far_ref[...]).astype(BF16)
    ogg_ref[...] = product(oc_ref[...], conv)

    take(p_all, 1, n - 1)
    scale = 1.0 / math.sqrt(rows * n)
    hop = jnp.exp(-float(rows) * fold)

    for b in range(n):
        pf_ref[b] = p_all[b].astype(F32)

    def owner(b, carry):
        s, far, first, second, near0, near1 = carry
        zero = one = jnp.zeros((modes, lanes), F32)
        for j in range(count):
            part = fold_ref[j] * pf_ref[b, j : j + 1, :]
            zero += part
            one += float(node[j]) * part
        d0 = pltpu.roll(zero, lanes - own, 1)
        d1 = pltpu.roll(one, lanes - own, 1)
        first += d0 * s
        second += (d0 + d1) * s + d0 * far
        return s * hop + zero, (far + rows * s) * hop + one, first, second, near0 + zero, near1 + one

    empty = jnp.zeros((modes, lanes), F32)
    _, _, first, second, near0, near1 = lax.fori_loop(0, n, owner, (empty,) * 6, unroll=8 if n % 8 == 0 else 1)
    step = jnp.exp(-fold)
    first = (step * first + pltpu.roll(near0, lanes - 2 * own, 1))[:, :own]
    second = (step * second + pltpu.roll(near1, lanes - 2 * own, 1))[:, :own]
    gain = jnp.sqrt(2.0 * mine / modes)
    rg_ref[...] = gain * first * scale
    tg_ref[...] = res_ref[...] * gain * (0.5 * first - mine * second) * scale

    @pl.when(me == n - 1)
    def _():
        dv_rim[...] = jnp.zeros_like(dv_rim)

    @pl.when(me < n - 1)
    def _():
        dv_copy(me).wait_recv()

    ws = ds_ref[...] + sign * spectrum(dv_rim[...])
    xg_ref[...] = signal(times(fs_ref[...], ws, True)).astype(BF16)

    pltpu.make_async_copy(unit_ref, unit_ref, all_sem.at[0]).wait()

    @pl.when(me < n - 1)
    def _():
        rim_copy(me + 1).wait_send()

    @pl.when(me > 0)
    def _():
        dv_copy(me - 1).wait_send()

    take(fg_all, 2, n - 1)
    total = jnp.sum(fg_all[...].astype(F32), axis=0) * scale
    for side in range(sides):
        fg_ref[side * few : (side + 1) * few, :] = total[side]


def store(*refs):
    count = (len(refs) - 1) // 2
    gives = [pltpu.make_async_copy(refs[i], refs[count + i], refs[-1].at[i]) for i in range(count)]
    for give in gives:
        give.start()
    for give in gives:
        give.wait()


def local(x, og, ig, oc, filt, res, rate):
    n = lax.axis_size(AXIS)
    rows, chans = x.shape
    modes, own = rate.shape
    groups = filt.shape[1]
    assert rows == filt.shape[0] and modes % 8 == 0 and 2 * (modes // 8) * own <= 128 and 128 % own == 0
    assert chans % 128 == 0 and n % (chans // 128) == 0
    sides = chans // 128
    fwd, inv, turn = dft_tables(rows)
    node, mom, up, lo, far = node_tables(rows)
    count = len(node)
    tall = mom.shape[0] // 2
    tab = np.concatenate([fwd, inv, turn, far, up])
    sent = 4 * 8 * 128 + 2 * (tall * 128 + groups * rows + tall * chans)
    hbm = pl.BlockSpec(memory_space=pltpu.HBM)
    vmem = pl.BlockSpec(memory_space=pltpu.VMEM)
    wide = (rows, chans)
    dma = pltpu.SemaphoreType.DMA
    out = pl.pallas_call(
        functools.partial(kernel, n, tuple(float(v) for v in node)),
        name="mixer",
        out_shape=(
            pltpu.VMEM(wide, BF16),
            pltpu.VMEM(wide, BF16),
            pltpu.VMEM(wide, BF16),
            pltpu.VMEM((groups, rows), F32),
            pltpu.VMEM((modes, own), F32),
            pltpu.VMEM((modes, own), F32),
        ),
        in_specs=[hbm] * 10,
        out_specs=(vmem,) * 6,
        scratch_shapes=[
            pltpu.VMEM(wide, BF16),
            pltpu.VMEM((8, 128), F32),
            pltpu.VMEM((n, 8, 128), F32),
            pltpu.VMEM((2, tall, chans), BF16),
            pltpu.VMEM((n, tall, chans), BF16),
            pltpu.VMEM(wide, BF16),
            pltpu.VMEM(wide, BF16),
            pltpu.VMEM((n, tall, 128), BF16),
            pltpu.VMEM((n, tall, 128), BF16),
            pltpu.VMEM((sides, groups // sides, rows), BF16),
            pltpu.VMEM((n, sides, groups // sides, rows), BF16),
            pltpu.VMEM((modes, chans), F32),
            pltpu.VMEM((modes, chans), F32),
            pltpu.VMEM((count, modes, 128), F32),
            pltpu.VMEM((n, tall, 128), F32),
            pltpu.VMEM((count, modes, chans), F32),
            pltpu.VMEM((tall, chans), F32),
            pltpu.VMEM((count,) + wide, F32),
            pltpu.VMEM((tall, chans), F32),
            pltpu.VMEM(wide, F32),
            pltpu.VMEM((8 * count, chans), F32),
            pltpu.VMEM((tall, chans), F32),
            pltpu.VMEM(wide, F32),
            pltpu.VMEM((2 * rows, chans), F32),
            pltpu.VMEM((2 * rows, chans), F32),
            pltpu.VMEM((2 * rows, chans), F32),
            pltpu.VMEM(wide, BF16),
            pltpu.VMEM(wide, BF16),
            pltpu.VMEM(wide, BF16),
            pltpu.VMEM((4,) + wide, BF16),
            pltpu.VMEM((groups, rows), BF16),
            pltpu.VMEM((2, modes, own), F32),
            pltpu.VMEM(mom.shape, BF16),
            pltpu.VMEM(tab.shape, BF16),
            pltpu.VMEM(lo.shape, BF16),
            pltpu.VMEM((n - 1, sent // 512, 128), F32),
            dma((7,)),
            dma((2,)), dma((2,)), dma((3 + sides,)), dma((n,)),
        ],
        compiler_params=pltpu.CompilerParams(
            collective_id=0, has_side_effects=True, vmem_limit_bytes=GRANT
        ),
    )(
        x, og, ig, oc, filt.T, res, rate,
        jnp.asarray(mom), jnp.asarray(tab), jnp.asarray(lo),
    )
    xg, ogg, igg, fg, rg, tg = pl.pallas_call(
        store,
        name="store",
        out_shape=tuple(jax.ShapeDtypeStruct(o.shape, o.dtype) for o in out),
        in_specs=[vmem] * 6,
        out_specs=(hbm,) * 6,
        scratch_shapes=[dma((6,))],
        compiler_params=pltpu.CompilerParams(vmem_limit_bytes=GRANT),
    )(*[pltpu.with_memory_space_constraint(o, pltpu.VMEM) for o in out])
    return xg, ogg, igg, fg.T, rg, tg


def solution(mesh):
    tokens = P("ctx", "ch")
    shared = P(None, "ch")
    owned = P(None, ("ch", "ctx"))
    return jax.shard_map(
        local,
        mesh=mesh,
        in_specs=(tokens, tokens, tokens, tokens, shared, owned, owned),
        out_specs=(tokens, tokens, tokens, shared, owned, owned),
        check_vma=False,
    )
```

time: 17.2 us -> 17 us (0.988)
  no operation moved by 1% of the time
where the time goes in v2:
time: 17 us; the launch traced here: 16.8 us
  Pallas kernels  16.2 us (95%)
  between operations  0.64 us (4%)
    pallas_call x1, Pallas kernels, local(): pl.pallas_call(functools.partial(kernel, n, tuple((float(v) for v in node...  15.4 us
    pallas_call x1, Pallas kernels, local(): pl.pallas_call(store, name='store', out_shape=tuple((jax.ShapeDtypeStruct...  0.73 us

profile of v2, /device:TPU:0, one launch (start us, length us, event | category | flops | bytes accessed | tf_op | source)
XLA Modules:
  0.0 16.8 jit_solution(12293806495042056041)
XLA Ops:
  0.6 15.4 %mixer.1 = (bf16[128,256]{1,0:T(8,128)(2,1)S(1)}, bf16[128,256]{1,0:T(8,128)(2,1)S(1)}, bf16[128,256]{1,0:T(8,128)(2,1)S(1)}, f32[16,128]{1,0:T(8,128)S(1)}, f32[16,32]{1,0:T(8,128)S(1)}, /*index=5*/f32[16,32]{1,0:T(8,128)S(1)}) custom-call(bf16[128,256]{1,0:T(8,128)(2,1)} %x_hbm.1, bf16[128,256]{1,0:T(8,128)(2,1)} %og_hbm.1, bf16[128,256]{1,0:T(8,128)(2,1)} %ig_hbm.1, ...), custom_call_target="tpu_custom_call" | custom-call | tf_op jit(solution)/shard_map/mixer/pallas_call | solution.py:498
  16.1 0.7 %store.1 = (bf16[128,256]{1,0:T(8,128)(2,1)}, bf16[128,256]{1,0:T(8,128)(2,1)}, bf16[128,256]{1,0:T(8,128)(2,1)}, f32[16,128]{1,0:T(8,128)}, f32[16,32]{1,0:T(8,128)}, /*index=5*/f32[16,32]{1,0:T(8,128)}) custom-call(bf16[128,256]{1,0:T(8,128)(2,1)S(1)} %get-tuple-element.18.refs_0_, bf16[128,256]{1,0:T(8,128)(2,1)S(1)} %get-tuple-element.19.refs_1_, ...), custom_call_target="tpu_custom_call" | custom-call | tf_op jit(solution)/shard_map/store/pallas_call | solution.py:558

commit v3 on v2

--- a/solution.py
+++ b/solution.py
@@ -163,8 +163,9 @@
     def p_copy(to):
         return remote(p_send.at[to], p_all.at[me], all_sem.at[0], all_sem.at[1], to)
 
-    def fg_copy(side, to):
-        return remote(fg_send.at[side], fg_all.at[me, side], all_sem.at[0], all_sem.at[2], to)
+    def fg_copy(low, top, to):
+        part = pl.ds(low, top - low)
+        return remote(fg_send.at[part], fg_all.at[me, part], all_sem.at[0], all_sem.at[2], to)
 
     def du_copy(which, slot, to):
         return remote(du_send.at[which], du_all.at[slot], all_sem.at[0], du_recv.at[slot], to)
@@ -195,10 +196,6 @@
     others(lambda j: rr_copy(j).start())
     span(0, me, lambda j: du_copy(0, me, j).start())
 
-    @pl.when(me < n - 1)
-    def _():
-        rim_copy(me + 1).start()
-
     rr_all[me] = rr_send[...]
     load(tab_hbm, tab_ref, 3).wait()
     far_at = 3 * size
@@ -206,18 +203,20 @@
     for j in range(count):
         b_ref[j] = dot(tab_ref[up_at + j * rows : up_at + (j + 1) * rows, :], dz2)
 
+    @pl.when(me < n - 1)
+    def _():
+        rim_copy(me + 1).start()
+
     load(filt_hbm, filt_ref, 5).wait()
     fwd = tab_ref[:size, :]
     inv_hi = tab_ref[size : size + rows, :]
-    inv_lo = tab_ref[size + rows : 2 * size, :]
     sign = (1 - 2 * lax.rem(lax.broadcasted_iota(jnp.int32, (size, chans), 0), 2)).astype(F32)
 
     def spectrum(value):
         return dot(fwd, twice(value))
 
     def signal(spec):
-        high, low = split(spec)
-        return dot(inv_hi, high) + dot(inv_hi, low) + dot(inv_lo, high)
+        return dot(inv_hi, spec.astype(BF16))
 
     def times(a, b, conj):
         ar, ai, br, bi = a[:rows], a[rows:], b[:rows], b[rows:]
@@ -307,18 +306,20 @@
     nt = (((1,), (1,)), ((), ()))
     few = groups // sides
     turn = tab_ref[2 * size : 3 * size, :]
-    def grad(side):
-        cols = slice(128 * side, 128 * side + 128)
-
-        @pl.when(me // crowd == side)
-        def _(side=side):
-            take(rr_all, 3 + side, crowd - 1)
-
-        @pl.when(me // crowd != side)
-        def _(side=side):
-            take(rr_all, 3 + side, crowd)
-
-        for j in range(side * crowd, (side + 1) * crowd):
+    def grad(low, top):
+        cols = slice(128 * low, 128 * top)
+
+        for side in reversed(range(low, top)):
+
+            @pl.when(me // crowd == side)
+            def _(side=side):
+                take(rr_all, 3 + side, crowd - 1)
+
+            @pl.when(me // crowd != side)
+            def _(side=side):
+                take(rr_all, 3 + side, crowd)
+
+        for j in range(low * crowd, top * crowd):
             piece = rr_all[j]
             for g in range(parts):
                 at = (slice(8 * g, 8 * g + 8), slice(j * own, (j + 1) * own))
@@ -333,11 +334,11 @@
             h_ref[j : j + 1, cols] = jnp.sum(weight * e, axis=0, keepdims=True)
 
         @pl.when(me < n - 1)
-        def _(side=side, cols=cols):
-            if side == sides - 1:
+        def _():
+            if top == sides:
                 span(me + 1, n, lambda j: du_copy(0, j, j).wait_recv())
             decay = jnp.exp(-rates[:, cols] * rows)
-            start = jnp.zeros((modes, 128), F32)
+            start = jnp.zeros((modes, 128 * (top - low)), F32)
             spread(
                 lax.fori_loop(0, n - 1 - me, lambda i, q: gather(n - 1 - i, q * decay, cols), start), 1, cols
             )
@@ -352,40 +353,46 @@
             back_ref[here, cols] = back
             dv[here, cols] = product(back, ig_ref[here, cols])
 
-    def tap(side):
-        cols = slice(128 * side, 128 * side + 128)
+    def tap(low, top):
+        cols = slice(128 * low, 128 * top)
         spec = spectrum(dv[:, cols])
         ds_ref[:, cols] = spec
         cross = times(xs_ref[:, cols], spec, True).astype(BF16)
-        sums = lax.dot_general(
-            member[side * few : (side + 1) * few, cols], cross, nt, preferred_element_type=F32
-        )
+        sums = lax.dot_general(member[low * few : top * few, cols], cross, nt, preferred_element_type=F32)
         both = dot(jnp.concatenate(split(sums), axis=0), turn)
-        fg_send[side] = (both[:few, :rows] + both[few:, :rows] + both[:few, rows:]).astype(BF16)
-        others(lambda j: fg_copy(side, j).start())
+        many = (top - low) * few
+        part = (both[:many, :rows] + both[many:, :rows] + both[:many, rows:]).astype(BF16)
+        for side in range(low, top):
+            fg_send[side] = part[(side - low) * few : (side - low + 1) * few]
+        others(lambda j: fg_copy(low, top, j).start())
 
     def hand():
         @pl.when(me > 0)
         def _():
             dv_copy(me - 1).start()
 
-    @pl.when(me >= n // 2)
+    @pl.when(me == n - 1)
     def _():
         mix()
         for side in reversed(range(sides)):
-            grad(side)
+            grad(side, side + 1)
             if side == 0:
                 hand()
-            tap(side)
+            tap(side, side + 1)
+
+    @pl.when((me >= n // 2) & (me < n - 1))
+    def _():
+        mix()
+        grad(0, sides)
+        hand()
+        tap(0, sides)
 
     @pl.when(me < n // 2)
     def _():
-        for side in reversed(range(sides)):
-            grad(side)
+        grad(0, sides)
         hand()
         mix()
-        for side in reversed(range(sides)):
-            tap(side)
+        tap(0, sides)
 
     fg_all[me] = fg_send[...]
     igg_ref[...] = product(back_ref[...], mr_ref[...])

time: 17 us -> 16.6 us (0.976)
  Pallas kernels: 16.2 us -> 15.7 us
    pallas_call x1, Pallas kernels: 15.4 us -> 15 us  [local(): pl.pallas_call(functools.partial(kernel, n, tuple((float(v) for v in node...]
where the time goes in v3:
time: 16.6 us; the launch traced here: 16.4 us
  Pallas kernels  15.7 us (95%)
  between operations  0.64 us (4%)
    pallas_call x1, Pallas kernels, local(): pl.pallas_call(functools.partial(kernel, n, tuple((float(v) for v in node...  15 us
    pallas_call x1, Pallas kernels, local(): pl.pallas_call(store, name='store', out_shape=tuple((jax.ShapeDtypeStruct...  0.73 us

profile of v3, /device:TPU:0, one launch (start us, length us, event | category | flops | bytes accessed | tf_op | source)
XLA Modules:
  0.0 16.4 jit_solution(9121239743742069224)
XLA Ops:
  0.6 15.0 %mixer.1 = (bf16[128,256]{1,0:T(8,128)(2,1)S(1)}, bf16[128,256]{1,0:T(8,128)(2,1)S(1)}, bf16[128,256]{1,0:T(8,128)(2,1)S(1)}, f32[16,128]{1,0:T(8,128)S(1)}, f32[16,32]{1,0:T(8,128)S(1)}, /*index=5*/f32[16,32]{1,0:T(8,128)S(1)}) custom-call(bf16[128,256]{1,0:T(8,128)(2,1)} %x_hbm.1, bf16[128,256]{1,0:T(8,128)(2,1)} %og_hbm.1, bf16[128,256]{1,0:T(8,128)(2,1)} %ig_hbm.1, ...), custom_call_target="tpu_custom_call" | custom-call | tf_op jit(solution)/shard_map/mixer/pallas_call | solution.py:505
  15.6 0.7 %store.1 = (bf16[128,256]{1,0:T(8,128)(2,1)}, bf16[128,256]{1,0:T(8,128)(2,1)}, bf16[128,256]{1,0:T(8,128)(2,1)}, f32[16,128]{1,0:T(8,128)}, f32[16,32]{1,0:T(8,128)}, /*index=5*/f32[16,32]{1,0:T(8,128)}) custom-call(bf16[128,256]{1,0:T(8,128)(2,1)S(1)} %get-tuple-element.18.refs_0_, bf16[128,256]{1,0:T(8,128)(2,1)S(1)} %get-tuple-element.19.refs_1_, ...), custom_call_target="tpu_custom_call" | custom-call | tf_op jit(solution)/shard_map/store/pallas_call | solution.py:565

commit v4 on v3

--- a/solution.py
+++ b/solution.py
@@ -104,7 +104,7 @@
     rim, rr_send, rr_all, du_send, du_all, dv, dv_rim, p_send, p_all, fg_send, fg_all,
     rates, resid, fold_ref, pf_ref, e_ref, h_ref, b_ref, row_ref, far_ref, pb_ref, g_ref,
     conv_ref, xs_ref, fs_ref, ds_ref, mr_ref, u_ref, back_ref,
-    wide_ref, filt_ref, own_ref, mom_ref, tab_ref, lo_ref, unit_ref, in_sem,
+    wide_ref, filt_ref, own_ref, tab_ref, unit_ref, in_sem,
     rim_sem, dv_sem, all_sem, du_recv,
 ):
     me = lax.axis_index(AXIS)
@@ -112,7 +112,7 @@
 
     def others(act):
         def step(k, carry):
-            act(lax.rem(me + k, n))
+            act(lax.rem(me + jnp.where(me < n // 2, n - k, k), n))
             return carry
 
         lax.fori_loop(1, n, step, 0)
@@ -129,25 +129,25 @@
     def load(src, dst, i):
         return pltpu.make_async_copy(src, dst, in_sem.at[i])
 
+    rows, chans = x_hbm.shape
+    wide = [wide_ref.at[pl.ds(i * rows, rows)] for i in range(4)]
+    og_ref, oc_ref, x_ref, ig_ref = wide
+    mom_ref = wide_ref.at[pl.ds(4 * rows, mom_hbm.shape[0])]
+    head = tab_hbm.shape[0]
     load(rate_hbm, own_ref.at[0], 0).start()
     load(res_hbm, own_ref.at[1], 0).start()
-    load(og_hbm, wide_ref.at[0], 1).start()
-    load(oc_hbm, wide_ref.at[1], 1).start()
-    load(mom_hbm, mom_ref, 2).start()
-    load(tab_hbm, tab_ref, 3).start()
-    load(x_hbm, wide_ref.at[2], 4).start()
-    load(ig_hbm, wide_ref.at[3], 4).start()
-    load(filt_hbm, filt_ref, 5).start()
-    load(lo_hbm, lo_ref, 6).start()
-    og_ref, oc_ref, x_ref, ig_ref = (wide_ref.at[i] for i in range(4))
+    for src, dst in zip((og_hbm, oc_hbm, x_hbm, ig_hbm, mom_hbm), wide + [mom_ref]):
+        load(src, dst, 1).start()
+    load(tab_hbm, tab_ref.at[pl.ds(0, head)], 2).start()
+    load(lo_hbm, tab_ref.at[pl.ds(head, lo_hbm.shape[0])], 2).start()
+    load(filt_hbm, filt_ref, 3).start()
     rate_ref, res_ref = own_ref.at[0], own_ref.at[1]
 
-    rows, chans = x_hbm.shape
     modes, own = rate_hbm.shape
     groups = filt_hbm.shape[0]
     parts = modes // 8
     count = len(node)
-    tall = mom_ref.shape[0] // 2
+    tall = mom_hbm.shape[0] // 2
     size = 2 * rows
     sides = chans // 128
     crowd = n // sides
@@ -168,46 +168,58 @@
         return remote(fg_send.at[part], fg_all.at[me, part], all_sem.at[0], all_sem.at[2], to)
 
     def du_copy(which, slot, to):
-        return remote(du_send.at[which], du_all.at[slot], all_sem.at[0], du_recv.at[slot], to)
+        return remote(du_send.at[which], du_all.at[slot], all_sem.at[0], du_recv.at[which], to)
 
     def rim_copy(to):
-        return remote(x_ref, rim, rim_sem.at[0], rim_sem.at[1], to)
+        return remote(x_ref, rim, all_sem.at[0], rim_sem.at[0], to)
 
     def dv_copy(to):
-        return remote(dv, dv_rim, dv_sem.at[0], dv_sem.at[1], to)
+        return remote(dv, dv_rim, all_sem.at[0], dv_sem.at[0], to)
 
     def take(ref, i, many):
         part = ref.at[pl.ds(0, many)]
         pltpu.make_async_copy(part, part, all_sem.at[i]).wait()
+
+    def arrive(which, many):
+        for exact in range(1, n):
+
+            @pl.when(many == exact)
+            def _(exact=exact):
+                part = du_all.at[pl.ds(0, exact)]
+                pltpu.make_async_copy(part, part, du_recv.at[which]).wait()
 
     p_send[...] = jnp.zeros_like(p_send)
     g_ref[...] = jnp.zeros_like(g_ref)
     load(own_ref, own_ref, 0).wait()
     for g in range(parts):
         rr_send[:, g * own : (g + 1) * own] = rate_ref[8 * g : 8 * g + 8, :]
-        rr_send[:, (parts + g) * own : (parts + g + 1) * own] = res_ref[8 * g : 8 * g + 8, :]
-
-    load(wide_ref.at[pl.ds(0, 2)], wide_ref.at[pl.ds(0, 2)], 1).wait()
-    load(mom_ref, mom_ref, 2).wait()
+        gain = jnp.sqrt(2.0 * rate_ref[8 * g : 8 * g + 8, :] / modes)
+        rr_send[:, (parts + g) * own : (parts + g + 1) * own] = res_ref[8 * g : 8 * g + 8, :] * gain
+
+    load(wide_ref, wide_ref, 1).wait()
     dz2 = twice(product(og_ref[...], oc_ref[...]))
     du_send[0] = dot(mom_ref[:tall, :], dz2).astype(BF16)
-    load(wide_ref.at[pl.ds(2, 2)], wide_ref.at[pl.ds(2, 2)], 4).wait()
     pl.semaphore_wait(barrier, n - 1)
     others(lambda j: rr_copy(j).start())
+
+    @pl.when((me >= n // 2 - 1) & (me < n - 1))
+    def _():
+        rim_copy(me + 1).start()
+
     span(0, me, lambda j: du_copy(0, me, j).start())
 
     rr_all[me] = rr_send[...]
-    load(tab_hbm, tab_ref, 3).wait()
+    load(tab_ref, tab_ref, 2).wait()
     far_at = 3 * size
     up_at = far_at + size
     for j in range(count):
         b_ref[j] = dot(tab_ref[up_at + j * rows : up_at + (j + 1) * rows, :], dz2)
 
-    @pl.when(me < n - 1)
+    @pl.when(me < n // 2 - 1)
     def _():
         rim_copy(me + 1).start()
 
-    load(filt_hbm, filt_ref, 5).wait()
+    load(filt_hbm, filt_ref, 3).wait()
     fwd = tab_ref[:size, :]
     inv_hi = tab_ref[size : size + rows, :]
     sign = (1 - 2 * lax.rem(lax.broadcasted_iota(jnp.int32, (size, chans), 0), 2)).astype(F32)
@@ -305,7 +317,7 @@
 
     nt = (((1,), (1,)), ((), ()))
     few = groups // sides
-    turn = tab_ref[2 * size : 3 * size, :]
+    turn = tab_ref[2 * size : 3 * size, :rows]
     def grad(low, top):
         cols = slice(128 * low, 128 * top)
 
@@ -326,8 +338,7 @@
                 rates[at] = piece[:, g * own : (g + 1) * own]
                 resid[at] = piece[:, (parts + g) * own : (parts + g + 1) * own]
         rate = rates[:, cols]
-        weight = resid[:, cols] * jnp.sqrt(2.0 * rate / modes)
-        resid[:, cols] = weight
+        weight = resid[:, cols]
         for j in range(count):
             e = jnp.exp(-float(node[j]) * rate)
             e_ref[j, :, cols] = e
@@ -336,7 +347,7 @@
         @pl.when(me < n - 1)
         def _():
             if top == sides:
-                span(me + 1, n, lambda j: du_copy(0, j, j).wait_recv())
+                arrive(0, n - 1 - me)
             decay = jnp.exp(-rates[:, cols] * rows)
             start = jnp.zeros((modes, 128 * (top - low)), F32)
             spread(
@@ -359,9 +370,7 @@
         ds_ref[:, cols] = spec
         cross = times(xs_ref[:, cols], spec, True).astype(BF16)
         sums = lax.dot_general(member[low * few : top * few, cols], cross, nt, preferred_element_type=F32)
-        both = dot(jnp.concatenate(split(sums), axis=0), turn)
-        many = (top - low) * few
-        part = (both[:many, :rows] + both[many:, :rows] + both[:many, rows:]).astype(BF16)
+        part = dot(sums.astype(BF16), turn).astype(BF16)
         for side in range(low, top):
             fg_send[side] = part[(side - low) * few : (side - low + 1) * few]
         others(lambda j: fg_copy(low, top, j).start())
@@ -380,14 +389,14 @@
                 hand()
             tap(side, side + 1)
 
-    @pl.when((me >= n // 2) & (me < n - 1))
+    @pl.when((me > n // 2) & (me < n - 1))
     def _():
         mix()
         grad(0, sides)
         hand()
         tap(0, sides)
 
-    @pl.when(me < n // 2)
+    @pl.when(me <= n // 2)
     def _():
         grad(0, sides)
         hand()
@@ -398,10 +407,9 @@
     igg_ref[...] = product(back_ref[...], mr_ref[...])
     u2 = twice(u_ref[...])
 
-    load(lo_hbm, lo_ref, 6).wait()
     conv = jnp.zeros((rows, chans), F32)
     for j in range(count):
-        conv += h_ref[j : j + 1, :] * dot(lo_ref[j * rows : (j + 1) * rows, :], u2)
+        conv += h_ref[j : j + 1, :] * dot(tab_ref[head + j * rows : head + (j + 1) * rows, :], u2)
     conv_ref[...] = conv
 
     @pl.when(me == 0)
@@ -410,7 +418,7 @@
 
     @pl.when(me > 0)
     def _():
-        span(0, me, lambda j: du_copy(1, j, j).wait_recv())
+        arrive(1, me)
         decay = jnp.exp(-rates[...] * rows)
         every = slice(0, chans)
         start = jnp.zeros((modes, chans), F32)
@@ -459,15 +467,17 @@
     ws = ds_ref[...] + sign * spectrum(dv_rim[...])
     xg_ref[...] = signal(times(fs_ref[...], ws, True)).astype(BF16)
 
-    pltpu.make_async_copy(unit_ref, unit_ref, all_sem.at[0]).wait()
-
-    @pl.when(me < n - 1)
-    def _():
-        rim_copy(me + 1).wait_send()
-
-    @pl.when(me > 0)
-    def _():
-        dv_copy(me - 1).wait_send()
+    edge = (me == 0) | (me == n - 1)
+    most = unit_ref.shape[0]
+
+    @pl.when(edge)
+    def _():
+        part = unit_ref.at[pl.ds(0, most - rows * chans // 256)]
+        pltpu.make_async_copy(part, part, all_sem.at[0]).wait()
+
+    @pl.when(jnp.logical_not(edge))
+    def _():
+        pltpu.make_async_copy(unit_ref, unit_ref, all_sem.at[0]).wait()
 
     take(fg_all, 2, n - 1)
     total = jnp.sum(fg_all[...].astype(F32), axis=0) * scale
@@ -490,7 +500,7 @@
     modes, own = rate.shape
     groups = filt.shape[1]
     assert rows == filt.shape[0] and modes % 8 == 0 and 2 * (modes // 8) * own <= 128 and 128 % own == 0
-    assert chans % 128 == 0 and n % (chans // 128) == 0
+    assert chans == 2 * rows and chans % 128 == 0 and n % (chans // 128) == 0
     sides = chans // 128
     fwd, inv, turn = dft_tables(rows)
     node, mom, up, lo, far = node_tables(rows)
@@ -545,15 +555,13 @@
             pltpu.VMEM(wide, BF16),
             pltpu.VMEM(wide, BF16),
             pltpu.VMEM(wide, BF16),
-            pltpu.VMEM((4,) + wide, BF16),
+            pltpu.VMEM((4 * rows + mom.shape[0], chans), BF16),
             pltpu.VMEM((groups, rows), BF16),
             pltpu.VMEM((2, modes, own), F32),
-            pltpu.VMEM(mom.shape, BF16),
-            pltpu.VMEM(tab.shape, BF16),
-            pltpu.VMEM(lo.shape, BF16),
-            pltpu.VMEM((n - 1, sent // 512, 128), F32),
-            dma((7,)),
-            dma((2,)), dma((2,)), dma((3 + sides,)), dma((n,)),
+            pltpu.VMEM((tab.shape[0] + lo.shape[0], 2 * rows), BF16),
+            pltpu.VMEM(((n - 1) * (sent // 512) + rows * chans // 128, 128), F32),
+            dma((4,)),
+            dma((1,)), dma((1,)), dma((3 + sides,)), dma((2,)),
         ],
         compiler_params=pltpu.CompilerParams(
             collective_id=0, has_side_effects=True, vmem_limit_bytes=GRANT

time: 16.6 us -> 16.3 us (0.982)
  Pallas kernels: 15.7 us -> 15.4 us
    pallas_call x1, Pallas kernels: 15 us -> 14.7 us  [local(): pl.pallas_call(functools.partial(kernel, n, tuple((float(v) for v in node...]
where the time goes in v4:
time: 16.3 us; the launch traced here: 16 us
  Pallas kernels  15.4 us (94%)
  between operations  0.64 us (4%)
    pallas_call x1, Pallas kernels, local(): pl.pallas_call(functools.partial(kernel, n, tuple((float(v) for v in node...  14.7 us
    pallas_call x1, Pallas kernels, local(): pl.pallas_call(store, name='store', out_shape=tuple((jax.ShapeDtypeStruct...  0.73 us

profile of v4, /device:TPU:0, one launch (start us, length us, event | category | flops | bytes accessed | tf_op | source)
XLA Modules:
  0.0 16.0 jit_solution(6871792691144479231)
XLA Ops:
  0.6 14.7 %mixer.1 = (bf16[128,256]{1,0:T(8,128)(2,1)S(1)}, bf16[128,256]{1,0:T(8,128)(2,1)S(1)}, bf16[128,256]{1,0:T(8,128)(2,1)S(1)}, f32[16,128]{1,0:T(8,128)S(1)}, f32[16,32]{1,0:T(8,128)S(1)}, /*index=5*/f32[16,32]{1,0:T(8,128)S(1)}) custom-call(bf16[128,256]{1,0:T(8,128)(2,1)} %x_hbm.1, bf16[128,256]{1,0:T(8,128)(2,1)} %og_hbm.1, bf16[128,256]{1,0:T(8,128)(2,1)} %ig_hbm.1, ...), custom_call_target="tpu_custom_call" | custom-call | tf_op jit(solution)/shard_map/mixer/pallas_call | solution.py:515
  15.3 0.7 %store.1 = (bf16[128,256]{1,0:T(8,128)(2,1)}, bf16[128,256]{1,0:T(8,128)(2,1)}, bf16[128,256]{1,0:T(8,128)(2,1)}, f32[16,128]{1,0:T(8,128)}, f32[16,32]{1,0:T(8,128)}, /*index=5*/f32[16,32]{1,0:T(8,128)}) custom-call(bf16[128,256]{1,0:T(8,128)(2,1)S(1)} %get-tuple-element.18.refs_0_, bf16[128,256]{1,0:T(8,128)(2,1)S(1)} %get-tuple-element.19.refs_1_, ...), custom_call_target="tpu_custom_call" | custom-call | tf_op jit(solution)/shard_map/store/pallas_call | solution.py:573

commit v5 on v4

--- a/solution.py
+++ b/solution.py
@@ -427,6 +427,17 @@
     conv = (conv_ref[...] + far_ref[...]).astype(BF16)
     ogg_ref[...] = product(oc_ref[...], conv)
 
+    @pl.when(me == n - 1)
+    def _():
+        dv_rim[...] = jnp.zeros_like(dv_rim)
+
+    @pl.when(me < n - 1)
+    def _():
+        dv_copy(me).wait_recv()
+
+    ws = ds_ref[...] + sign * spectrum(dv_rim[...])
+    xg_ref[...] = signal(times(fs_ref[...], ws, True)).astype(BF16)
+
     take(p_all, 1, n - 1)
     scale = 1.0 / math.sqrt(rows * n)
     hop = jnp.exp(-float(rows) * fold)
@@ -455,17 +466,6 @@
     gain = jnp.sqrt(2.0 * mine / modes)
     rg_ref[...] = gain * first * scale
     tg_ref[...] = res_ref[...] * gain * (0.5 * first - mine * second) * scale
-
-    @pl.when(me == n - 1)
-    def _():
-        dv_rim[...] = jnp.zeros_like(dv_rim)
-
-    @pl.when(me < n - 1)
-    def _():
-        dv_copy(me).wait_recv()
-
-    ws = ds_ref[...] + sign * spectrum(dv_rim[...])
-    xg_ref[...] = signal(times(fs_ref[...], ws, True)).astype(BF16)
 
     edge = (me == 0) | (me == n - 1)
     most = unit_ref.shape[0]

time: 16.3 us -> 16.3 us (level)
  no operation moved by 1% of the time
where the time goes in v5:
time: 16.3 us; the launch traced here: 16 us
  Pallas kernels  15.4 us (94%)
  between operations  0.64 us (4%)
    pallas_call x1, Pallas kernels, local(): pl.pallas_call(functools.partial(kernel, n, tuple((float(v) for v in node...  14.7 us
    pallas_call x1, Pallas kernels, local(): pl.pallas_call(store, name='store', out_shape=tuple((jax.ShapeDtypeStruct...  0.73 us

profile of v5, /device:TPU:0, one launch (start us, length us, event | category | flops | bytes accessed | tf_op | source)
XLA Modules:
  0.0 16.0 jit_solution(18091487641678478049)
XLA Ops:
  0.6 14.7 %mixer.1 = (bf16[128,256]{1,0:T(8,128)(2,1)S(1)}, bf16[128,256]{1,0:T(8,128)(2,1)S(1)}, bf16[128,256]{1,0:T(8,128)(2,1)S(1)}, f32[16,128]{1,0:T(8,128)S(1)}, f32[16,32]{1,0:T(8,128)S(1)}, /*index=5*/f32[16,32]{1,0:T(8,128)S(1)}) custom-call(bf16[128,256]{1,0:T(8,128)(2,1)} %x_hbm.1, bf16[128,256]{1,0:T(8,128)(2,1)} %og_hbm.1, bf16[128,256]{1,0:T(8,128)(2,1)} %ig_hbm.1, ...), custom_call_target="tpu_custom_call" | custom-call | tf_op jit(solution)/shard_map/mixer/pallas_call | solution.py:515
  15.3 0.7 %store.1 = (bf16[128,256]{1,0:T(8,128)(2,1)}, bf16[128,256]{1,0:T(8,128)(2,1)}, bf16[128,256]{1,0:T(8,128)(2,1)}, f32[16,128]{1,0:T(8,128)}, f32[16,32]{1,0:T(8,128)}, /*index=5*/f32[16,32]{1,0:T(8,128)}) custom-call(bf16[128,256]{1,0:T(8,128)(2,1)S(1)} %get-tuple-element.18.refs_0_, bf16[128,256]{1,0:T(8,128)(2,1)S(1)} %get-tuple-element.19.refs_1_, ...), custom_call_target="tpu_custom_call" | custom-call | tf_op jit(solution)/shard_map/store/pallas_call | solution.py:573

commit v6 on v5

--- a/solution.py
+++ b/solution.py
@@ -268,6 +268,10 @@
         state = dot(mom_ref[tall:, :], u2).astype(BF16)
         du_send[1] = state
         span(me + 1, n, lambda j: du_copy(1, me, j).start())
+
+    def share():
+        u = u_ref[...]
+        state = du_send[1]
         for j in range(count):
             total = jnp.zeros((8, chans), F32)
             for t in range(rows // 8):
@@ -383,25 +387,44 @@
     @pl.when(me == n - 1)
     def _():
         mix()
+        share()
         for side in reversed(range(sides)):
             grad(side, side + 1)
             if side == 0:
                 hand()
             tap(side, side + 1)
 
-    @pl.when((me > n // 2) & (me < n - 1))
+    @pl.when(me == n - 2)
     def _():
         mix()
+        share()
         grad(0, sides)
         hand()
         tap(0, sides)
 
-    @pl.when(me <= n // 2)
+    @pl.when((me > n // 2) & (me < n - 2))
+    def _():
+        mix()
+        share()
+        grad(0, sides)
+        hand()
+        tap(0, sides)
+
+    @pl.when((me == n // 2) & (me < n - 2))
+    def _():
+        grad(0, sides)
+        hand()
+        mix()
+        share()
+        tap(0, sides)
+
+    @pl.when((me < n // 2) & (me < n - 2))
     def _():
         grad(0, sides)
         hand()
         mix()
         tap(0, sides)
+        share()
 
     fg_all[me] = fg_send[...]
     igg_ref[...] = product(back_ref[...], mr_ref[...])
@@ -486,12 +509,12 @@
 
 
 def store(*refs):
-    count = (len(refs) - 1) // 2
-    gives = [pltpu.make_async_copy(refs[i], refs[count + i], refs[-1].at[i]) for i in range(count)]
-    for give in gives:
-        give.start()
-    for give in gives:
-        give.wait()
+    sources, targets, (wide, small, sem) = refs[:6], refs[6:12], refs[12:]
+    for source, target, which in zip(sources, targets, (0, 0, 0, 1, 2, 2)):
+        pltpu.make_async_copy(source, target, sem.at[which]).start()
+    pltpu.make_async_copy(wide, wide, sem.at[0]).wait()
+    pltpu.make_async_copy(sources[3], targets[3], sem.at[1]).wait()
+    pltpu.make_async_copy(small, small, sem.at[2]).wait()
 
 
 def local(x, og, ig, oc, filt, res, rate):
@@ -576,7 +599,7 @@
         out_shape=tuple(jax.ShapeDtypeStruct(o.shape, o.dtype) for o in out),
         in_specs=[vmem] * 6,
         out_specs=(hbm,) * 6,
-        scratch_shapes=[dma((6,))],
+        scratch_shapes=[pltpu.VMEM((3,) + wide, BF16), pltpu.VMEM((2, modes, own), F32), dma((3,))],
         compiler_params=pltpu.CompilerParams(vmem_limit_bytes=GRANT),
     )(*[pltpu.with_memory_space_constraint(o, pltpu.VMEM) for o in out])
     return xg, ogg, igg, fg.T, rg, tg

time: 16.3 us -> 16.2 us (level)
  no operation moved by 1% of the time
where the time goes in v6:
time: 16.2 us; the launch traced here: 16 us
  Pallas kernels  15.4 us (95%)
  between operations  0.64 us (4%)
    pallas_call x1, Pallas kernels, local(): pl.pallas_call(functools.partial(kernel, n, tuple((float(v) for v in node...  14.7 us
    pallas_call x1, Pallas kernels, local(): pl.pallas_call(store, name='store', out_shape=tuple((jax.ShapeDtypeStruct...  0.71 us

profile of v6, /device:TPU:0, one launch (start us, length us, event | category | flops | bytes accessed | tf_op | source)
XLA Modules:
  0.0 16.0 jit_solution(9038507874121023311)
XLA Ops:
  0.6 14.7 %mixer.1 = (bf16[128,256]{1,0:T(8,128)(2,1)S(1)}, bf16[128,256]{1,0:T(8,128)(2,1)S(1)}, bf16[128,256]{1,0:T(8,128)(2,1)S(1)}, f32[16,128]{1,0:T(8,128)S(1)}, f32[16,32]{1,0:T(8,128)S(1)}, /*index=5*/f32[16,32]{1,0:T(8,128)S(1)}) custom-call(bf16[128,256]{1,0:T(8,128)(2,1)} %x_hbm.1, bf16[128,256]{1,0:T(8,128)(2,1)} %og_hbm.1, bf16[128,256]{1,0:T(8,128)(2,1)} %ig_hbm.1, ...), custom_call_target="tpu_custom_call" | custom-call | tf_op jit(solution)/shard_map/mixer/pallas_call | solution.py:538
  15.3 0.7 %store.1 = (bf16[128,256]{1,0:T(8,128)(2,1)}, bf16[128,256]{1,0:T(8,128)(2,1)}, bf16[128,256]{1,0:T(8,128)(2,1)}, f32[16,128]{1,0:T(8,128)}, f32[16,32]{1,0:T(8,128)}, /*index=5*/f32[16,32]{1,0:T(8,128)}) custom-call(bf16[128,256]{1,0:T(8,128)(2,1)S(1)} %get-tuple-element.18.refs_0_, bf16[128,256]{1,0:T(8,128)(2,1)S(1)} %get-tuple-element.19.refs_1_, ...), custom_call_target="tpu_custom_call" | custom-call | tf_op jit(solution)/shard_map/store/pallas_call | solution.py:596

commit v7 on v6

--- a/solution.py
+++ b/solution.py
@@ -225,7 +225,7 @@
     sign = (1 - 2 * lax.rem(lax.broadcasted_iota(jnp.int32, (size, chans), 0), 2)).astype(F32)
 
     def spectrum(value):
-        return dot(fwd, twice(value))
+        return dot(fwd[:, :rows], value)
 
     def signal(spec):
         return dot(inv_hi, spec.astype(BF16))
@@ -390,25 +390,24 @@
         share()
         for side in reversed(range(sides)):
             grad(side, side + 1)
-            if side == 0:
-                hand()
             tap(side, side + 1)
+        hand()
 
     @pl.when(me == n - 2)
     def _():
         mix()
         share()
         grad(0, sides)
+        tap(0, sides)
         hand()
-        tap(0, sides)
 
     @pl.when((me > n // 2) & (me < n - 2))
     def _():
         mix()
         share()
         grad(0, sides)
+        tap(0, sides)
         hand()
-        tap(0, sides)
 
     @pl.when((me == n // 2) & (me < n - 2))
     def _():

time: 16.2 us -> 16.2 us (level)
  no operation moved by 1% of the time
where the time goes in v7:
time: 16.2 us; the launch traced here: 16 us
  Pallas kernels  15.3 us (94%)
  between operations  0.64 us (4%)
    pallas_call x1, Pallas kernels, local(): pl.pallas_call(functools.partial(kernel, n, tuple((float(v) for v in node...  14.6 us
    pallas_call x1, Pallas kernels, local(): pl.pallas_call(store, name='store', out_shape=tuple((jax.ShapeDtypeStruct...  0.71 us

profile of v7, /device:TPU:0, one launch (start us, length us, event | category | flops | bytes accessed | tf_op | source)
XLA Modules:
  0.0 16.0 jit_solution(5928199908415786610)
XLA Ops:
  0.6 14.6 %mixer.1 = (bf16[128,256]{1,0:T(8,128)(2,1)S(1)}, bf16[128,256]{1,0:T(8,128)(2,1)S(1)}, bf16[128,256]{1,0:T(8,128)(2,1)S(1)}, f32[16,128]{1,0:T(8,128)S(1)}, f32[16,32]{1,0:T(8,128)S(1)}, /*index=5*/f32[16,32]{1,0:T(8,128)S(1)}) custom-call(bf16[128,256]{1,0:T(8,128)(2,1)} %x_hbm.1, bf16[128,256]{1,0:T(8,128)(2,1)} %og_hbm.1, bf16[128,256]{1,0:T(8,128)(2,1)} %ig_hbm.1, ...), custom_call_target="tpu_custom_call" | custom-call | tf_op jit(solution)/shard_map/mixer/pallas_call | solution.py:537
  15.3 0.7 %store.1 = (bf16[128,256]{1,0:T(8,128)(2,1)}, bf16[128,256]{1,0:T(8,128)(2,1)}, bf16[128,256]{1,0:T(8,128)(2,1)}, f32[16,128]{1,0:T(8,128)}, f32[16,32]{1,0:T(8,128)}, /*index=5*/f32[16,32]{1,0:T(8,128)}) custom-call(bf16[128,256]{1,0:T(8,128)(2,1)S(1)} %get-tuple-element.18.refs_0_, bf16[128,256]{1,0:T(8,128)(2,1)S(1)} %get-tuple-element.19.refs_1_, ...), custom_call_target="tpu_custom_call" | custom-call | tf_op jit(solution)/shard_map/store/pallas_call | solution.py:595

commit v8 on v7

--- a/solution.py
+++ b/solution.py
@@ -412,10 +412,10 @@
     @pl.when((me == n // 2) & (me < n - 2))
     def _():
         grad(0, sides)
-        hand()
         mix()
         share()
         tap(0, sides)
+        hand()
 
     @pl.when((me < n // 2) & (me < n - 2))
     def _():

time: 16.2 us -> 16.2 us (level)
  no operation moved by 1% of the time
where the time goes in v8:
time: 16.2 us; the launch traced here: 16 us
  Pallas kernels  15.3 us (94%)
  between operations  0.64 us (4%)
    pallas_call x1, Pallas kernels, local(): pl.pallas_call(functools.partial(kernel, n, tuple((float(v) for v in node...  14.6 us
    pallas_call x1, Pallas kernels, local(): pl.pallas_call(store, name='store', out_shape=tuple((jax.ShapeDtypeStruct...  0.71 us

profile of v8, /device:TPU:0, one launch (start us, length us, event | category | flops | bytes accessed | tf_op | source)
XLA Modules:
  0.0 16.0 jit_solution(10065970392750024819)
XLA Ops:
  0.6 14.6 %mixer.1 = (bf16[128,256]{1,0:T(8,128)(2,1)S(1)}, bf16[128,256]{1,0:T(8,128)(2,1)S(1)}, bf16[128,256]{1,0:T(8,128)(2,1)S(1)}, f32[16,128]{1,0:T(8,128)S(1)}, f32[16,32]{1,0:T(8,128)S(1)}, /*index=5*/f32[16,32]{1,0:T(8,128)S(1)}) custom-call(bf16[128,256]{1,0:T(8,128)(2,1)} %x_hbm.1, bf16[128,256]{1,0:T(8,128)(2,1)} %og_hbm.1, bf16[128,256]{1,0:T(8,128)(2,1)} %ig_hbm.1, ...), custom_call_target="tpu_custom_call" | custom-call | tf_op jit(solution)/shard_map/mixer/pallas_call | solution.py:537
  15.3 0.7 %store.1 = (bf16[128,256]{1,0:T(8,128)(2,1)}, bf16[128,256]{1,0:T(8,128)(2,1)}, bf16[128,256]{1,0:T(8,128)(2,1)}, f32[16,128]{1,0:T(8,128)}, f32[16,32]{1,0:T(8,128)}, /*index=5*/f32[16,32]{1,0:T(8,128)}) custom-call(bf16[128,256]{1,0:T(8,128)(2,1)S(1)} %get-tuple-element.18.refs_0_, bf16[128,256]{1,0:T(8,128)(2,1)S(1)} %get-tuple-element.19.refs_1_, ...), custom_call_target="tpu_custom_call" | custom-call | tf_op jit(solution)/shard_map/store/pallas_call | solution.py:595
